TPU v7x, 128 devices: a whole 4x4x4 slice. The times are simulated.
128 devices in a mesh: dev: 128 (over y, x, z, core).
Axes of the slice: x: 4, y: 4, z: 4, core: 2. Of those that a mesh axis runs over, the one named last changes fastest.
Arguments:
- embeddings: bfloat16 [32768, 1024], P('dev'), may hold values from -6 to 6
- cluster_id: int32 [32768], P('dev'), may hold values from 0 to 15, as said below
- requests: int32 [16384], P('dev'), may hold values from -1 to 1, as said below
- pair_left: int32 [49152], P('dev'), may hold values from 0 to 127, as said below
- pair_right: int32 [49152], P('dev'), may hold values from 0 to 127, as said below
Outputs:
- best: float32 [32768], P('dev')
Inputs may be any that keep to these rules, and one draw needn't show every extreme that they name: Rows are sorted by cluster: cluster_id never falls along the rows, and every cluster has rows. Every slot that some task of device d names has a block (requests at least 0 there); a device's tasks name slots of at most 40 consecutive owners. pair_left <= pair_right for every task; no device lists one slot pair twice. `pair_right`: see pair_left.
All inputs are finite; a program needn't handle non-finite values.
Results may differ from a plain program's by a relative error of at most 0.00086.
Values may be sent and summed in bfloat16 or wider, within the bound.
A program may use at most 192 MiB of HBM per device.

v0:
```python
import jax
import jax.numpy as jnp
from jax import lax
from jax.sharding import PartitionSpec as P

D = 1024
BLOCK = 128
GROUP = 64


def local(embeddings, cluster_id, requests, pair_left, pair_right):
    devices = lax.axis_size("dev")
    blk_dev = embeddings.shape[0] // BLOCK
    values = embeddings.astype(jnp.float32)
    unit = (values * lax.rsqrt(jnp.sum(values * values, axis=-1, keepdims=True) + 1e-06)).astype(
        jnp.bfloat16
    )
    unit = unit.reshape(blk_dev, BLOCK, D)
    labels = cluster_id.reshape(blk_dev, BLOCK)
    asked = lax.all_to_all(requests, "dev", split_axis=0, concat_axis=0, tiled=True)
    picked = jnp.clip(asked, 0, blk_dev - 1)
    outgoing = unit[picked]
    out_labels = labels[picked].astype(jnp.bfloat16)
    fetched, fetched_labels = (
        lax.all_to_all(outgoing, "dev", split_axis=0, concat_axis=0, tiled=True),
        lax.all_to_all(out_labels, "dev", split_axis=0, concat_axis=0, tiled=True),
    )
    fetched_labels = fetched_labels.astype(jnp.int32)
    diagonal_mask = jnp.eye(BLOCK, dtype=bool)

    def step(carry, indices):
        left, right = indices
        sims = jnp.einsum(
            "gid,gjd->gij", fetched[left], fetched[right], preferred_element_type=jnp.float32
        )
        same = fetched_labels[left][:, :, None] == fetched_labels[right][:, None, :]
        selfish = (left == right)[:, None, None] & diagonal_mask[None]
        sims = jnp.where(same & ~selfish, sims, jnp.float32(-1.0))
        carry = carry.at[left].max(jnp.max(sims, axis=2))
        carry = carry.at[right].max(jnp.max(sims, axis=1))
        return (carry, None)

    start = jnp.full((devices, BLOCK), -1.0, jnp.float32)
    slot_best, _ = lax.scan(
        step, start, (pair_left.reshape(-1, GROUP), pair_right.reshape(-1, GROUP))
    )
    returned = lax.all_to_all(slot_best, "dev", split_axis=0, concat_axis=0, tiled=True)
    masked = jnp.where((asked >= 0)[:, None], returned, jnp.float32(-1.0))
    result = jnp.full((blk_dev, BLOCK), -1.0, jnp.float32).at[picked].max(masked)
    return result.reshape(-1)


def solution(mesh):
    in_specs = (P("dev", None), P("dev"), P("dev"), P("dev"), P("dev"))
    out_specs = P("dev")
    return jax.shard_map(local, mesh=mesh, in_specs=in_specs, out_specs=out_specs, check_vma=False)
```

profile of v0, /device:TPU:1, one launch (start us, length us, event | category | flops | bytes accessed | tf_op | source)
XLA Modules:
  0.0 860.3 jit_solution(6005790251280296125)
XLA Ops:
  1.4 11.5 %all-to-all-start = ((s32[128,1,1]{2,1,0:T(1,128)}), s32[128,1,1]{2,1,0:T(1,128)S(1)}, u32[]{:S(2)}, u32[]{:S(2)}) async-start(s32[128,1,1]{2,1,0:T(1,128)} %copy.8), calls=%async_computation | async-start | bytes 131072 | tf_op jit(solution)/shard_map/all_to_all | solution.py:20
  14.1 8.2 all-to-all-done
  22.3 2.4 clamp_reduce_fusion
  26.6 4.6 all-to-all-start.1
  32.4 12.2 %gather_fusion.5 = bf16[128,128,1024]{2,1,0:T(8,128)(2,1)} fusion(bf16[2,128,1024]{2,1,0:T(8,128)(2,1)S(1)} %bitcast.36, s32[1024]{0:T(1024)S(1)} %pad_clamp_fusion.2), kind=kCustom, calls=%fused_computation.5 | custom fusion | bytes 67109376 | tf_op jit(solution)/shard_map/gather | solution.py:22
  44.6 10.4 %all-to-all-start.2 = ((bf16[128,128,1024]{2,1,0:T(8,128)(2,1)}), bf16[128,128,1024]{2,1,0:T(8,128)(2,1)}, u32[]{:S(2)}, u32[]{:S(2)}) async-start(bf16[128,128,1024]{2,1,0:T(8,128)(2,1)} %gather_fusion.5), calls=%async_computation.2 | async-start | bytes 67108864 | tf_op jit(solution)/shard_map/all_to_all | solution.py:25
  55.3 476.9 %all-to-all-done.2 = bf16[128,128,1024]{2,1,0:T(8,128)(2,1)} async-done(((bf16[128,128,1024]{2,1,0:T(8,128)(2,1)}), bf16[128,128,1024]{2,1,0:T(8,128)(2,1)}, u32[]{:S(2)}, u32[]{:S(2)}) %all-to-all-start.2) | async-done | bytes 33554464 | tf_op jit(solution)/shard_map/all_to_all | solution.py:25
  532.9 276.0 %while.11 = (s32[]{:T(128)}, f32[128,128]{1,0:T(8,128)}, s32[6,64]{1,0:T(8,128)S(1)}, s32[128,128]{1,0:T(8,128)S(1)}, s32[6,64]{1,0:T(8,128)S(1)}, /*index=5*/bf16[128,128,1024]{2,1,0:T(8,128)(2,1)}, s32[]{:T(128)}) while((s32[]{:T(128)}, f32[128,128]{1,0:T(8,128)}, s32[6,64]{1,0:T(8,128)S(1)}, s32[128,128]{1,0:T(8,128)S(1)}, ...), condition=%wide.region_6.7_spmd.clone, body=%wide.region_1.6_spmd.clone.sunk | while | flops 2154842624 | bytes 101166816 | solution.py:44
  534.2 13.9 %gather_fusion.2 = bf16[64,128,1024]{2,1,0:T(8,128)(2,1)} fusion(bf16[128,128,1024]{2,1,0:T(8,128)(2,1)} %get-tuple-element.137, s32[1024]{0:T(1024)S(1)} %pad_clamp_fusion.6), kind=kCustom, calls=%fused_computation.2.clone.clone.1 | custom fusion | bytes 33554688 | tf_op jit(solution)/shard_map/while/body/eval_jaxpr/gather | solution.py:34
  548.1 14.2 %gather_fusion.3 = bf16[64,128,1024]{2,1,0:T(8,128)(2,1)} fusion(bf16[128,128,1024]{2,1,0:T(8,128)(2,1)} %get-tuple-element.137, s32[1024]{0:T(1024)S(1)} %pad_clamp_fusion.5), kind=kCustom, calls=%fused_computation.3.clone.clone.1 | custom fusion | bytes 33554688 | tf_op jit(solution)/shard_map/while/body/eval_jaxpr/gather | solution.py:34
  562.3 13.1 %fusion.23 = (f32[64,128]{1,0:T(8,128)S(1)}, f32[64,128]{1,0:T(8,128)S(1)}) fusion(s32[64,128]{1,0:T(8,128)S(1)} %gather_fusion, s32[64,128]{1,0:T(8,128)S(1)} %gather_fusion.1, pred[128,128]{1,0:T(8,128)(4,1)S(1)} %iota_compare_fusion.2, pred[64]{0:T(512)(128)(4,1)S(1)} %compare_bitcast_fusion.2, bf16[64,128,1024]{2,1,0:T(8,128)(2,1)} %gather_fusion.2, ...), kind=kOutput, calls=%fused_computation.11.clone.1 | convolution fusion | flops 2154807296 | bytes 33701952 | tf_op jit(solution)/shard_map/while/body/eval_jaxpr/gid,gjd->gij/dot_general | solution.py:33
  575.4 2.3 scatter_fusion
  581.2 14.3 %gather_fusion.2 = bf16[64,128,1024]{2,1,0:T(8,128)(2,1)} fusion(bf16[128,128,1024]{2,1,0:T(8,128)(2,1)} %get-tuple-element.137, s32[1024]{0:T(1024)S(1)} %pad_clamp_fusion.6), kind=kCustom, calls=%fused_computation.2.clone.clone.1 | custom fusion | bytes 33554688 | tf_op jit(solution)/shard_map/while/body/eval_jaxpr/gather | solution.py:34
  595.5 13.1 %gather_fusion.3 = bf16[64,128,1024]{2,1,0:T(8,128)(2,1)} fusion(bf16[128,128,1024]{2,1,0:T(8,128)(2,1)} %get-tuple-element.137, s32[1024]{0:T(1024)S(1)} %pad_clamp_fusion.5), kind=kCustom, calls=%fused_computation.3.clone.clone.1 | custom fusion | bytes 33554688 | tf_op jit(solution)/shard_map/while/body/eval_jaxpr/gather | solution.py:34
  608.6 13.1 %fusion.23 = (f32[64,128]{1,0:T(8,128)S(1)}, f32[64,128]{1,0:T(8,128)S(1)}) fusion(s32[64,128]{1,0:T(8,128)S(1)} %gather_fusion, s32[64,128]{1,0:T(8,128)S(1)} %gather_fusion.1, pred[128,128]{1,0:T(8,128)(4,1)S(1)} %iota_compare_fusion.2, pred[64]{0:T(512)(128)(4,1)S(1)} %compare_bitcast_fusion.2, bf16[64,128,1024]{2,1,0:T(8,128)(2,1)} %gather_fusion.2, ...), kind=kOutput, calls=%fused_computation.11.clone.1 | convolution fusion | flops 2154807296 | bytes 33701952 | tf_op jit(solution)/shard_map/while/body/eval_jaxpr/gid,gjd->gij/dot_general | solution.py:33
  621.7 2.3 scatter_fusion
  627.5 14.0 %gather_fusion.2 = bf16[64,128,1024]{2,1,0:T(8,128)(2,1)} fusion(bf16[128,128,1024]{2,1,0:T(8,128)(2,1)} %get-tuple-element.137, s32[1024]{0:T(1024)S(1)} %pad_clamp_fusion.6), kind=kCustom, calls=%fused_computation.2.clone.clone.1 | custom fusion | bytes 33554688 | tf_op jit(solution)/shard_map/while/body/eval_jaxpr/gather | solution.py:34
  641.5 12.8 %gather_fusion.3 = bf16[64,128,1024]{2,1,0:T(8,128)(2,1)} fusion(bf16[128,128,1024]{2,1,0:T(8,128)(2,1)} %get-tuple-element.137, s32[1024]{0:T(1024)S(1)} %pad_clamp_fusion.5), kind=kCustom, calls=%fused_computation.3.clone.clone.1 | custom fusion | bytes 33554688 | tf_op jit(solution)/shard_map/while/body/eval_jaxpr/gather | solution.py:34
  654.4 13.1 %fusion.23 = (f32[64,128]{1,0:T(8,128)S(1)}, f32[64,128]{1,0:T(8,128)S(1)}) fusion(s32[64,128]{1,0:T(8,128)S(1)} %gather_fusion, s32[64,128]{1,0:T(8,128)S(1)} %gather_fusion.1, pred[128,128]{1,0:T(8,128)(4,1)S(1)} %iota_compare_fusion.2, pred[64]{0:T(512)(128)(4,1)S(1)} %compare_bitcast_fusion.2, bf16[64,128,1024]{2,1,0:T(8,128)(2,1)} %gather_fusion.2, ...), kind=kOutput, calls=%fused_computation.11.clone.1 | convolution fusion | flops 2154807296 | bytes 33701952 | tf_op jit(solution)/shard_map/while/body/eval_jaxpr/gid,gjd->gij/dot_general | solution.py:33
  667.5 2.3 scatter_fusion
  673.3 12.7 %gather_fusion.2 = bf16[64,128,1024]{2,1,0:T(8,128)(2,1)} fusion(bf16[128,128,1024]{2,1,0:T(8,128)(2,1)} %get-tuple-element.137, s32[1024]{0:T(1024)S(1)} %pad_clamp_fusion.6), kind=kCustom, calls=%fused_computation.2.clone.clone.1 | custom fusion | bytes 33554688 | tf_op jit(solution)/shard_map/while/body/eval_jaxpr/gather | solution.py:34
  686.0 12.8 %gather_fusion.3 = bf16[64,128,1024]{2,1,0:T(8,128)(2,1)} fusion(bf16[128,128,1024]{2,1,0:T(8,128)(2,1)} %get-tuple-element.137, s32[1024]{0:T(1024)S(1)} %pad_clamp_fusion.5), kind=kCustom, calls=%fused_computation.3.clone.clone.1 | custom fusion | bytes 33554688 | tf_op jit(solution)/shard_map/while/body/eval_jaxpr/gather | solution.py:34
  698.8 13.1 %fusion.23 = (f32[64,128]{1,0:T(8,128)S(1)}, f32[64,128]{1,0:T(8,128)S(1)}) fusion(s32[64,128]{1,0:T(8,128)S(1)} %gather_fusion, s32[64,128]{1,0:T(8,128)S(1)} %gather_fusion.1, pred[128,128]{1,0:T(8,128)(4,1)S(1)} %iota_compare_fusion.2, pred[64]{0:T(512)(128)(4,1)S(1)} %compare_bitcast_fusion.2, bf16[64,128,1024]{2,1,0:T(8,128)(2,1)} %gather_fusion.2, ...), kind=kOutput, calls=%fused_computation.11.clone.1 | convolution fusion | flops 2154807296 | bytes 33701952 | tf_op jit(solution)/shard_map/while/body/eval_jaxpr/gid,gjd->gij/dot_general | solution.py:33
  717.8 14.0 %gather_fusion.2 = bf16[64,128,1024]{2,1,0:T(8,128)(2,1)} fusion(bf16[128,128,1024]{2,1,0:T(8,128)(2,1)} %get-tuple-element.137, s32[1024]{0:T(1024)S(1)} %pad_clamp_fusion.6), kind=kCustom, calls=%fused_computation.2.clone.clone.1 | custom fusion | bytes 33554688 | tf_op jit(solution)/shard_map/while/body/eval_jaxpr/gather | solution.py:34
  731.8 13.1 %gather_fusion.3 = bf16[64,128,1024]{2,1,0:T(8,128)(2,1)} fusion(bf16[128,128,1024]{2,1,0:T(8,128)(2,1)} %get-tuple-element.137, s32[1024]{0:T(1024)S(1)} %pad_clamp_fusion.5), kind=kCustom, calls=%fused_computation.3.clone.clone.1 | custom fusion | bytes 33554688 | tf_op jit(solution)/shard_map/while/body/eval_jaxpr/gather | solution.py:34
  744.9 13.1 %fusion.23 = (f32[64,128]{1,0:T(8,128)S(1)}, f32[64,128]{1,0:T(8,128)S(1)}) fusion(s32[64,128]{1,0:T(8,128)S(1)} %gather_fusion, s32[64,128]{1,0:T(8,128)S(1)} %gather_fusion.1, pred[128,128]{1,0:T(8,128)(4,1)S(1)} %iota_compare_fusion.2, pred[64]{0:T(512)(128)(4,1)S(1)} %compare_bitcast_fusion.2, bf16[64,128,1024]{2,1,0:T(8,128)(2,1)} %gather_fusion.2, ...), kind=kOutput, calls=%fused_computation.11.clone.1 | convolution fusion | flops 2154807296 | bytes 33701952 | tf_op jit(solution)/shard_map/while/body/eval_jaxpr/gid,gjd->gij/dot_general | solution.py:33
  763.8 12.9 %gather_fusion.2 = bf16[64,128,1024]{2,1,0:T(8,128)(2,1)} fusion(bf16[128,128,1024]{2,1,0:T(8,128)(2,1)} %get-tuple-element.137, s32[1024]{0:T(1024)S(1)} %pad_clamp_fusion.6), kind=kCustom, calls=%fused_computation.2.clone.clone.1 | custom fusion | bytes 33554688 | tf_op jit(solution)/shard_map/while/body/eval_jaxpr/gather | solution.py:34
  776.8 14.4 %gather_fusion.3 = bf16[64,128,1024]{2,1,0:T(8,128)(2,1)} fusion(bf16[128,128,1024]{2,1,0:T(8,128)(2,1)} %get-tuple-element.137, s32[1024]{0:T(1024)S(1)} %pad_clamp_fusion.5), kind=kCustom, calls=%fused_computation.3.clone.clone.1 | custom fusion | bytes 33554688 | tf_op jit(solution)/shard_map/while/body/eval_jaxpr/gather | solution.py:34
  791.2 13.1 %fusion.23 = (f32[64,128]{1,0:T(8,128)S(1)}, f32[64,128]{1,0:T(8,128)S(1)}) fusion(s32[64,128]{1,0:T(8,128)S(1)} %gather_fusion, s32[64,128]{1,0:T(8,128)S(1)} %gather_fusion.1, pred[128,128]{1,0:T(8,128)(4,1)S(1)} %iota_compare_fusion.2, pred[64]{0:T(512)(128)(4,1)S(1)} %compare_bitcast_fusion.2, bf16[64,128,1024]{2,1,0:T(8,128)(2,1)} %gather_fusion.2, ...), kind=kOutput, calls=%fused_computation.11.clone.1 | convolution fusion | flops 2154807296 | bytes 33701952 | tf_op jit(solution)/shard_map/while/body/eval_jaxpr/gid,gjd->gij/dot_general | solution.py:33
  808.9 39.8 %all-to-all-start.3 = ((f32[128,1,128]{2,1,0:T(1,128)}), f32[128,1,128]{2,1,0:T(1,128)S(1)}, u32[]{:S(2)}, u32[]{:S(2)}) async-start(f32[128,1,128]{2,1,0:T(1,128)} %bitcast.6), calls=%async_computation.3 | async-start | bytes 131072 | tf_op jit(solution)/shard_map/all_to_all | solution.py:47
  848.6 2.4 compare_reduce_fusion
  851.0 7.1 all-to-all-done.3
  (80 shorter events, 36.8 us)
Async XLA Ops:
  0.0 25.3 %copy-start = (s32[256]{0:T(256)S(1)}, s32[256]{0:T(256)}, u32[]{:S(2)}) copy-start(s32[256]{0:T(256)} %param.8) | copy-start | bytes 3076
  1.4 20.9 %all-to-all-start = ((s32[128,1,1]{2,1,0:T(1,128)}), s32[128,1,1]{2,1,0:T(1,128)S(1)}, u32[]{:S(2)}, u32[]{:S(2)}) async-start(s32[128,1,1]{2,1,0:T(1,128)} %copy.8), calls=%async_computation | async-start | bytes 131072 | tf_op jit(solution)/shard_map/all_to_all | solution.py:20
  22.3 4.3 copy-start.2
  24.7 0.6 copy-start.6
  26.6 18.0 %all-to-all-start.1 = ((bf16[128,1,128]{2,1,0:T(2,128)(2,1)}), bf16[128,1,128]{2,1,0:T(2,128)(2,1)S(1)}, u32[]{:S(2)}, u32[]{:S(2)}) async-start(bf16[128,1,128]{2,1,0:T(2,128)(2,1)} %copy.9), calls=%async_computation.1 | async-start | bytes 131072 | tf_op jit(solution)/shard_map/all_to_all | solution.py:26
  44.6 10.5 %copy-start.4 = (s32[384]{0:T(512)S(1)}, s32[384]{0:T(512)}, u32[]{:S(2)}) copy-start(s32[384]{0:T(512)} %param.10) | copy-start | bytes 4612
  44.6 10.6 %copy-start.5 = (s32[384]{0:T(512)S(1)}, s32[384]{0:T(512)}, u32[]{:S(2)}) copy-start(s32[384]{0:T(512)} %param.11) | copy-start | bytes 4612
  44.6 487.6 %all-to-all-start.2 = ((bf16[128,128,1024]{2,1,0:T(8,128)(2,1)}), bf16[128,128,1024]{2,1,0:T(8,128)(2,1)}, u32[]{:S(2)}, u32[]{:S(2)}) async-start(bf16[128,128,1024]{2,1,0:T(8,128)(2,1)} %gather_fusion.5), calls=%async_computation.2 | async-start | bytes 67108864 | tf_op jit(solution)/shard_map/all_to_all | solution.py:25
  532.9 315.8 %copy-start.3 = (s32[128,1,1]{2,1,0:T(1,128)S(1)}, s32[128,1,1]{2,1,0:T(1,128)}, u32[]{:S(2)}) copy-start(s32[128,1,1]{2,1,0:T(1,128)} %copy-done.2) | copy-start | bytes 1540
  808.9 51.4 %copy-start.1 = (s32[256]{0:T(256)S(1)}, s32[256]{0:T(256)}, u32[]{:S(2)}) copy-start(s32[256]{0:T(256)} %param.8) | copy-start | bytes 3076
  808.9 49.2 %all-to-all-start.3 = ((f32[128,1,128]{2,1,0:T(1,128)}), f32[128,1,128]{2,1,0:T(1,128)S(1)}, u32[]{:S(2)}, u32[]{:S(2)}) async-start(f32[128,1,128]{2,1,0:T(1,128)} %bitcast.6), calls=%async_computation.3 | async-start | bytes 131072 | tf_op jit(solution)/shard_map/all_to_all | solution.py:47
where the time goes:
time: 861 us; the launch traced here: 860 us
  waiting for transfers between devices  492 us (57%)
  local copies, waits for them, and re-layouts  186 us (22%)
  matrix products  78.5 us (9%)
  starting transfers between devices  66.3 us (8%)
  other arithmetic  37.1 us (4%)
    all_to_all x1, waiting for transfers between devices, local(): lax.all_to_all(outgoing, 'dev', split_axis=0, concat_axis=0, tiled=True)  477 us
    gather x6, local copies, waits for them, and re-layouts, step(): fetched[left]  81.9 us
    gather x6, local copies, waits for them, and re-layouts, step(): fetched[right]  80.5 us
    dot_general x6, matrix products, step(): jnp.einsum('gid,gjd->gij', fetched[left], fetched[right], preferred_eleme...  78.5 us
    all_to_all x1, starting transfers between devices, local(): lax.all_to_all(slot_best, 'dev', split_axis=0, concat_axis=0, tiled=True)  39.8 us
  transfers between devices with their start and end apart: 4, of which 3 were waited for; matrix products, arithmetic and copies ran while one was open for 2% of the time, Pallas kernels for 0%

commit v1 on v0

v1 whole, which is shorter than its diff:
```python
import functools

import jax
import jax.numpy as jnp
from jax import lax
from jax.experimental import pallas as pl
from jax.experimental.pallas import tpu as pltpu
from jax.sharding import PartitionSpec as P

BLOCK = 128
LINES = 16
DELTAS = (-1, 4, -3, 5, -2)
NV = len(DELTAS)
MESH = pl.DeviceIdType.MESH
F32 = jnp.float32
BF16 = jnp.bfloat16


def iota(shape, axis):
    return lax.broadcasted_iota(jnp.int32, shape, axis)


def dot_nt(a, b):
    return lax.dot_general(a, b, (((1,), (1,)), ((), ())), preferred_element_type=F32)


def dot_nn(a, b):
    return lax.dot_general(a, b, (((1,), (0,)), ((), ())), preferred_element_type=F32)


def onehot(mask):
    return jnp.where(mask, F32(1.0), F32(0.0)).astype(BF16)


def kernel(
    emb_ref, lab_ref, req_ref, pl_ref, pr_ref, out_ref,
    line, vis, wout, win, pout, pin, lcol, elab, racc, cacc, rout, rin, cout, cin,
    z_send, z_recv, p_send, p_recv, v_send, v_recv, w_send, w_recv, q_send, q_recv,
    r_send, r_recv, c_send, c_recv,
):
    rows = emb_ref.shape[0]
    half = rows // 2
    me = lax.axis_index("dev")
    core = lax.rem(me, 2)
    z = lax.rem(me // 2, 4)
    ln = me // 8

    def dev(dl, dz, dk):
        to_l = lax.rem(ln + dl + LINES, LINES)
        to_z = lax.rem(z + dz, 4)
        to_k = lax.rem(core + dk, 2)
        return to_l * 8 + to_z * 2 + to_k

    barrier = pltpu.get_barrier_semaphore()
    peers = [dev(0, s % 4, s // 4) for s in range(1, 8)] + [dev(j, 0, 0) for j in range(1, LINES)]
    for peer in peers:
        pl.semaphore_signal(barrier, inc=1, device_id=(peer,), device_id_type=MESH)

    def remote(src, dst, send, recv, to):
        return pltpu.make_async_remote_copy(
            src_ref=src, dst_ref=dst, send_sem=send, recv_sem=recv, device_id=(to,), device_id_type=MESH
        )

    @pl.loop(0, rows // 64)
    def _(i):
        at = pl.ds(pl.multiple_of(i * 64, 64), 64)
        x = emb_ref[at, :].astype(F32)
        total = jnp.sum(x * x, axis=1, keepdims=True)
        line[0, at, :] = (x * lax.rsqrt(total + 1e-06)).astype(BF16)

    expand = onehot((iota((256, 128), 0) // 2 == iota((256, 128), 1)) & (req_ref[...] == iota((256, 128), 0) % 2))
    left = dot_nn(expand, onehot(iota((128, pl_ref.shape[1]), 0) == pl_ref[...])).astype(BF16)
    right = dot_nn(expand, onehot(iota((128, pr_ref.shape[1]), 0) == pr_ref[...])).astype(BF16)
    want = (dot_nt(left, right) + dot_nt(right, left)).astype(BF16)
    labels = jnp.broadcast_to(lab_ref[...].astype(F32), (16, rows)).astype(BF16)
    for j in range(LINES):
        wout[j, 0:16, :] = want[16 * j : 16 * j + 16, :]
        wout[j, 16:32, :] = labels

    pl.semaphore_wait(barrier, len(peers))

    up_a = remote(line.at[0, 0:half], line.at[3, 0:half], z_send.at[0], z_recv.at[0], dev(0, 1, 0))
    dn_b = remote(line.at[0, half:rows], line.at[1, half:rows], z_send.at[1], z_recv.at[1], dev(0, 3, 0))
    up_b = remote(line.at[0, half:rows], line.at[3, half:rows], z_send.at[2], z_recv.at[2], dev(0, 1, 0))
    dn_a = remote(line.at[0, 0:half], line.at[1, 0:half], z_send.at[3], z_recv.at[3], dev(0, 3, 0))
    far_a = remote(line.at[3, 0:half], line.at[2, 0:half], z_send.at[4], z_recv.at[4], dev(0, 1, 0))
    far_b = remote(line.at[1, half:rows], line.at[2, half:rows], z_send.at[5], z_recv.at[5], dev(0, 3, 0))
    share = [
        remote(line.at[r], line.at[4 + r], p_send.at[r], p_recv.at[r], dev(0, 0, 1)) for r in range(4)
    ]
    visits = [
        remote(
            line.at[0] if d != -2 else vis.at[DELTAS.index(-1)],
            vis.at[m], v_send.at[m], v_recv.at[m],
            dev(-d if d != -2 else 1, 0, 0),
        )
        for m, d in enumerate(DELTAS)
    ]
    tell = [
        remote(
            wout.at[lax.rem(ln + j, LINES)], win.at[LINES - j], w_send.at[j], w_recv.at[LINES - j], dev(j, 0, 0)
        )
        for j in range(1, LINES)
    ]
    back = [(4 - s % 4) % 4 + 4 * (s // 4) for s in range(8)]
    pool = [
        remote(pout, pin.at[back[s]], q_send.at[s], q_recv.at[back[s]], dev(0, s % 4, s // 4)) for s in range(1, 8)
    ]

    for copy in tell:
        copy.start()
    up_a.start()
    dn_b.start()
    share[0].start()
    up_b.start()
    dn_a.start()
    for m, d in enumerate(DELTAS):
        if d != -2:
            visits[m].start()

    total = wout[ln, 0:16, :].astype(F32)
    for copy in tell:
        copy.wait_recv()
    for j in range(1, LINES):
        total = total + win[j, 0:16, :].astype(F32)
    pout[0:16, :] = total.astype(BF16)
    pout[16:32, :] = labels
    for copy in pool:
        copy.start()

    up_a.wait_recv()
    far_a.start()
    dn_b.wait_recv()
    far_b.start()

    for copy in pool:
        copy.wait_recv()
    for s in range(1, 8):
        total = total + pin[s, 0:16, :].astype(F32)
    total = total.astype(BF16)

    eye = iota((BLOCK, BLOCK), 0) == iota((BLOCK, BLOCK), 1)
    ones = jnp.full((BLOCK, BLOCK), 1.0, BF16)
    for s in range(8):
        row = labels[0:1, :] if s == 0 else pin[s, 16:32, :][0:1, :]
        for h in range(2):
            diag = jnp.where(eye, jnp.broadcast_to(row[:, h * BLOCK : (h + 1) * BLOCK].astype(F32), (BLOCK, BLOCK)), F32(0.0))
            lcol[2 * s + h] = dot_nn(diag.astype(BF16), ones)

    for m in range(NV + 1):
        d = 0 if m == 0 else DELTAS[m - 1]
        owner = dev(d, 0, 0)
        pick = onehot(iota((256, rows), 0) == owner * 2 + iota((256, rows), 1) // BLOCK)
        listed = dot_nn(total, pick)
        mine = (labels if m == 0 else win[d % LINES, 16:32, :]).astype(F32)
        elab[m] = jnp.where(listed > 0.5, mine, F32(-1.0))

    visits[DELTAS.index(-1)].wait_recv()
    visits[DELTAS.index(-2)].start()
    up_b.wait_recv()
    share[3].start()
    dn_a.wait_recv()
    share[1].start()
    far_a.wait_recv()
    far_b.wait_recv()
    share[2].start()

    racc[...] = jnp.full(racc.shape, -1.0, F32)

    def tile(m, s, rhs):
        sims = dot_nt(line[s], rhs[...])
        base = (lax.rem(z + s % 4, 4) * 2 + lax.rem(core + s // 4, 2)) * 2
        cols = []
        for h in range(2):
            lc = lcol[2 * s + h]
            tags = elab[m, pl.ds(base + h, 1), :]
            best = None
            parts = []
            for q in range(2):
                at = slice(q * BLOCK, (q + 1) * BLOCK)
                same = lc == tags[:, at]
                if m == 0 and h == q:
                    same = same & jnp.logical_not(eye & (s == 0))
                val = jnp.where(same, sims[h * BLOCK : (h + 1) * BLOCK, at], F32(-1.0))
                best = val if best is None else jnp.maximum(best, val)
                parts.append(jnp.max(val.reshape(16, 8, BLOCK), axis=0))
            if m > 0:
                racc[2 * s + h] = jnp.maximum(racc[2 * s + h], best)
            cols.append(jnp.concatenate(parts, axis=1))
        cacc[m] = jnp.maximum(cacc[m], jnp.maximum(cols[0], cols[1]))

    def column(m, rhs):
        cacc[m] = jnp.full(cacc.shape[1:], -1.0, F32)

        @pl.loop(0, 8)
        def _(s):
            tile(m, s, rhs)

        top = jnp.max(cacc[m], axis=0, keepdims=True)
        cout[m, 0:1, :] = top[:, 0:BLOCK]
        cout[m, 1:2, :] = top[:, BLOCK:]

    for copy in share:
        copy.wait_recv()
    column(0, line.at[0])
    give = []
    for m, d in enumerate(DELTAS):
        if d != -1:
            visits[m].wait_recv()
        column(m + 1, vis.at[m])
        copy = remote(cout.at[m + 1], cin.at[m], c_send.at[m], c_recv.at[m], dev(d, 0, 0))
        copy.start()
        give.append(copy)

    order = [1, 2, 3, 4, 5, 6, 7, 0]
    for s in order:
        for h in range(2):
            flat = jnp.max(jnp.transpose(racc[2 * s + h]), axis=0, keepdims=True)
            rout[s, h : h + 1, :] = flat
        if s > 0:
            copy = remote(rout.at[s], rin.at[back[s]], r_send.at[s], r_recv.at[back[s]], dev(0, s % 4, s // 4))
            copy.start()
            give.append(copy)

    result = jnp.maximum(rout[0], cout[0])
    for copy in give:
        copy.wait_recv()
    for m in range(NV):
        result = jnp.maximum(result, cin[m])
    for s in range(1, 8):
        result = jnp.maximum(result, rin[s])
    out_ref[...] = result
    for copy in [up_a, up_b, dn_a, dn_b, far_a, far_b] + share + visits + tell + pool + give:
        copy.wait_send()


def local(embeddings, cluster_id, requests, pair_left, pair_right):
    rows, width = embeddings.shape
    dma = pltpu.SemaphoreType.DMA
    vmem = pltpu.VMEM
    scratch = [
        vmem((8, rows, width), BF16),
        vmem((NV, rows, width), BF16),
        vmem((LINES, 32, 256), BF16),
        vmem((LINES, 32, 256), BF16),
        vmem((32, 256), BF16),
        vmem((8, 32, 256), BF16),
        vmem((16, BLOCK, BLOCK), F32),
        vmem((NV + 1, 16, rows), F32),
        vmem((16, BLOCK, BLOCK), F32),
        vmem((NV + 1, 8, rows), F32),
        vmem((8, 2, BLOCK), F32),
        vmem((8, 2, BLOCK), F32),
        vmem((NV + 1, 2, BLOCK), F32),
        vmem((NV, 2, BLOCK), F32),
    ]
    for count in (6, 4, NV, LINES, 8, 8, NV):
        scratch += [dma((count,)), dma((count,))]
    best = pl.pallas_call(
        kernel,
        out_shape=jax.ShapeDtypeStruct((2, BLOCK), F32),
        in_specs=[pl.BlockSpec(memory_space=pltpu.VMEM)] * 5,
        out_specs=pl.BlockSpec(memory_space=pltpu.VMEM),
        scratch_shapes=scratch,
        compiler_params=pltpu.CompilerParams(
            collective_id=0, has_side_effects=True, vmem_limit_bytes=48 * 1024 * 1024
        ),
        name="band",
    )(
        embeddings,
        cluster_id.reshape(1, -1),
        requests.reshape(1, -1),
        pair_left.reshape(1, -1),
        pair_right.reshape(1, -1),
    )
    return best.reshape(-1)


def solution(mesh):
    in_specs = (P("dev", None), P("dev"), P("dev"), P("dev"), P("dev"))
    out_specs = P("dev")
    return jax.shard_map(local, mesh=mesh, in_specs=in_specs, out_specs=out_specs, check_vma=False)
```

time: 861 us -> 79.6 us (0.09)
  waiting for transfers between devices: 492 us -> 0 us
  local copies, waits for them, and re-layouts: 186 us -> 3.65 us
  matrix products: 78.5 us -> 0 us
  Pallas kernels: 0 us -> 75.8 us
  starting transfers between devices: 66.3 us -> 0 us
  other arithmetic: 37.1 us -> 0 us
    all_to_all x4 -> x0, waiting for transfers between devices: 492 us -> none  [the longest x1 477 us: local(): lax.all_to_all(outgoing, 'dev', split_axis=0, concat_axis=0, tiled=True)]
    gather x26 -> x0, local copies, waits for them, and re-layouts: 182 us -> none  [the longest x6 81.9 us: step(): fetched[left]]
    dot_general x6 -> x0, matrix products: 78.5 us -> none  [step(): jnp.einsum('gid,gjd->gij', fetched[left], fetched[right], preferred_eleme...]
    pallas_call x0 -> x1, Pallas kernels: none -> 75.8 us  [local(): pl.pallas_call(kernel, out_shape=jax.ShapeDtypeStruct((2, BLOCK), F32), i...]
    all_to_all x4 -> x0, starting transfers between devices: 66.3 us -> none  [the longest x1 39.8 us: local(): lax.all_to_all(slot_best, 'dev', split_axis=0, concat_axis=0, tiled=True)]
    another operation x13 -> x0, other arithmetic: 29.6 us -> none  [the longest x6 13.7 us: step(): carry = carry.at[left].max(jnp.max(sims, axis=2))]
  transfers between devices with their start and end apart: 4 -> 0, of which waited for: 3 -> 0; matrix products, arithmetic and copies ran while one was open for 2% -> 0% of each run, Pallas kernels for 0% -> 0%
where the time goes in v1:
time: 79.6 us; the launch traced here: 79.4 us
  Pallas kernels  75.8 us (95%)
  local copies, waits for them, and re-layouts  3.65 us (5%)
    pallas_call x1, Pallas kernels, local(): pl.pallas_call(kernel, out_shape=jax.ShapeDtypeStruct((2, BLOCK), F32), i...  75.8 us
    unnamed x11, local copies, waits for them, and re-layouts  3.64 us

profile of v1, /device:TPU:1, one launch (start us, length us, event | category | flops | bytes accessed | tf_op | source)
XLA Modules:
  0.0 79.4 jit_solution(531697342232451914)
XLA Ops:
  0.0 0.0 copy-start.3
  0.0 0.7 copy-done.3
  0.7 0.0 copy-start.4
  0.7 0.7 copy-done.4
  1.4 0.0 copy-start.1
  1.4 0.0 copy-start.2
  1.4 0.7 copy-done.1
  2.0 0.0 copy-done.2
  2.0 0.0 copy-start
  2.0 1.0 %copy-done = bf16[256,1024]{1,0:T(8,128)(2,1)S(1)} copy-done((bf16[256,1024]{1,0:T(8,128)(2,1)S(1)}, bf16[256,1024]{1,0:T(8,128)(2,1)}, u32[]{:S(2)}) %copy-start) | copy-done | bytes 524312
  3.1 75.8 %band.1 = f32[2,128]{1,0:T(2,128)S(1)} custom-call(bf16[256,1024]{1,0:T(8,128)(2,1)S(1)} %copy-done, s32[1,256]{1,0:T(1,128)S(1)} %bitcast.4, s32[1,128]{1,0:T(1,128)S(1)} %bitcast.5, s32[1,384]{1,0:T(1,128)S(1)} %reshape.17.pl_ref, s32[1,384]{1,0:T(1,128)S(1)} %reshape.18.pr_ref), custom_call_target="tpu_custom_call" | custom-call | tf_op jit(solution)/shard_map/band/pallas_call | solution.py:259
  78.9 0.6 copy.7
  (2 shorter events, 0.0 us)
Async XLA Ops:
  0.0 0.7 copy-start.3
  0.7 0.7 copy-start.4
  1.4 0.7 copy-start.1
  1.4 0.7 copy-start.2
  2.0 1.0 %copy-start = (bf16[256,1024]{1,0:T(8,128)(2,1)S(1)}, bf16[256,1024]{1,0:T(8,128)(2,1)}, u32[]{:S(2)}) copy-start(bf16[256,1024]{1,0:T(8,128)(2,1)} %emb_ref.1) | copy-start | bytes 1572868

commit v2 on v1

--- a/solution.py
+++ b/solution.py
@@ -9,8 +9,31 @@
 
 BLOCK = 128
 LINES = 16
-DELTAS = (-1, 4, -3, 5, -2)
+DELTAS = (4, 1, 3, 5, 2)
 NV = len(DELTAS)
+CHUNKS = 2
+SPREAD = (
+    (0, 0, 0, -1, 4),
+    (1, 0, -1, 0, 1),
+    (1, 0, 0, -1, 4),
+    (2, 0, -1, 0, 1),
+    (2, 0, 0, -1, 4),
+    (3, 0, 1, 0, 3),
+    (3, 0, -1, 0, 1),
+    (3, 0, 0, -1, 4),
+    (0, 4, 1, 0, 3),
+    (0, 4, -1, 0, 1),
+    (1, 4, 1, 0, 3),
+    (2, 4, 1, 0, 3),
+    (3, 4, -1, 0, 5),
+    (0, 1, 0, -1, 5),
+    (1, 1, -1, 0, 2),
+    (1, 1, 0, -1, 5),
+    (2, 1, -1, 0, 2),
+    (3, 1, 0, -1, 5),
+    (1, 3, 1, 0, 2),
+    (2, 3, 1, 0, 2),
+)
 MESH = pl.DeviceIdType.MESH
 F32 = jnp.float32
 BF16 = jnp.bfloat16
@@ -88,14 +111,32 @@
     share = [
         remote(line.at[r], line.at[4 + r], p_send.at[r], p_recv.at[r], dev(0, 0, 1)) for r in range(4)
     ]
-    visits = [
-        remote(
-            line.at[0] if d != -2 else vis.at[DELTAS.index(-1)],
-            vis.at[m], v_send.at[m], v_recv.at[m],
-            dev(-d if d != -2 else 1, 0, 0),
-        )
-        for m, d in enumerate(DELTAS)
-    ]
+    x = lax.rem(ln, 4)
+    y = ln // 4
+    piece = rows // CHUNKS
+
+    def visit(number, part):
+        at, held, dx, dy, becomes = SPREAD[number]
+        rows_of = pl.ds(part * piece, piece)
+        src = line.at[0, rows_of] if held == 0 else vis.at[DELTAS.index(held), rows_of]
+        m = DELTAS.index(becomes)
+        to = (lax.rem(y + dy + 4, 4) * 4 + lax.rem(at + dx + 4, 4)) * 8 + z * 2 + core
+        return remote(src, vis.at[m, rows_of], v_send.at[number, part], v_recv.at[m, part], to)
+
+    def spread(held, part):
+        for c in range(4):
+            numbers = [n for n, entry in enumerate(SPREAD) if entry[0] == c and entry[1] == held]
+            if numbers:
+
+                @pl.when(x == c)
+                def _():
+                    for n in numbers:
+                        visit(n, part).start()
+
+    def arrive(delta, part):
+        number = [e[4] for e in SPREAD].index(delta)
+        visit(number, part).wait_recv()
+
     tell = [
         remote(
             wout.at[lax.rem(ln + j, LINES)], win.at[LINES - j], w_send.at[j], w_recv.at[LINES - j], dev(j, 0, 0)
@@ -114,9 +155,8 @@
     share[0].start()
     up_b.start()
     dn_a.start()
-    for m, d in enumerate(DELTAS):
-        if d != -2:
-            visits[m].start()
+    for part in range(CHUNKS):
+        spread(0, part)
 
     total = wout[ln, 0:16, :].astype(F32)
     for copy in tell:
@@ -128,6 +168,8 @@
     for copy in pool:
         copy.start()
 
+    arrive(4, 0)
+    spread(4, 0)
     up_a.wait_recv()
     far_a.start()
     dn_b.wait_recv()
@@ -155,12 +197,17 @@
         mine = (labels if m == 0 else win[d % LINES, 16:32, :]).astype(F32)
         elab[m] = jnp.where(listed > 0.5, mine, F32(-1.0))
 
-    visits[DELTAS.index(-1)].wait_recv()
-    visits[DELTAS.index(-2)].start()
+    for part in range(1, CHUNKS):
+        arrive(4, part)
+        spread(4, part)
     up_b.wait_recv()
     share[3].start()
     dn_a.wait_recv()
     share[1].start()
+    for delta in (1, 3):
+        for part in range(CHUNKS):
+            arrive(delta, part)
+            spread(delta, part)
     far_a.wait_recv()
     far_b.wait_recv()
     share[2].start()
@@ -192,7 +239,7 @@
     def column(m, rhs):
         cacc[m] = jnp.full(cacc.shape[1:], -1.0, F32)
 
-        @pl.loop(0, 8)
+        @pl.loop(0, 8, unroll=8)
         def _(s):
             tile(m, s, rhs)
 
@@ -205,8 +252,9 @@
     column(0, line.at[0])
     give = []
     for m, d in enumerate(DELTAS):
-        if d != -1:
-            visits[m].wait_recv()
+        if d in (5, 2):
+            for part in range(CHUNKS):
+                arrive(d, part)
         column(m + 1, vis.at[m])
         copy = remote(cout.at[m + 1], cin.at[m], c_send.at[m], c_recv.at[m], dev(d, 0, 0))
         copy.start()
@@ -230,8 +278,16 @@
     for s in range(1, 8):
         result = jnp.maximum(result, rin[s])
     out_ref[...] = result
-    for copy in [up_a, up_b, dn_a, dn_b, far_a, far_b] + share + visits + tell + pool + give:
+    for copy in [up_a, up_b, dn_a, dn_b, far_a, far_b] + share + tell + pool + give:
         copy.wait_send()
+    for c in range(4):
+
+        @pl.when(x == c)
+        def _():
+            for n, entry in enumerate(SPREAD):
+                if entry[0] == c:
+                    for part in range(CHUNKS):
+                        visit(n, part).wait_send()
 
 
 def local(embeddings, cluster_id, requests, pair_left, pair_right):
@@ -254,8 +310,16 @@
         vmem((NV + 1, 2, BLOCK), F32),
         vmem((NV, 2, BLOCK), F32),
     ]
-    for count in (6, 4, NV, LINES, 8, 8, NV):
-        scratch += [dma((count,)), dma((count,))]
+    for sent, received in (
+        ((6,), (6,)),
+        ((4,), (4,)),
+        ((len(SPREAD), CHUNKS), (NV, CHUNKS)),
+        ((LINES,), (LINES,)),
+        ((8,), (8,)),
+        ((8,), (8,)),
+        ((NV,), (NV,)),
+    ):
+        scratch += [dma(sent), dma(received)]
     best = pl.pallas_call(
         kernel,
         out_shape=jax.ShapeDtypeStruct((2, BLOCK), F32),

time: 79.6 us -> 53.3 us (0.67)
  Pallas kernels: 75.8 us -> 49.2 us
    pallas_call x1, Pallas kernels: 75.8 us -> 49.2 us  [local(): pl.pallas_call(kernel, out_shape=jax.ShapeDtypeStruct((2, BLOCK), F32), i...]
where the time goes in v2:
time: 53.3 us; the launch traced here: 52.9 us
  Pallas kernels  49.2 us (92%)
  local copies, waits for them, and re-layouts  3.65 us (7%)
    pallas_call x1, Pallas kernels, local(): pl.pallas_call(kernel, out_shape=jax.ShapeDtypeStruct((2, BLOCK), F32), i...  49.2 us
    unnamed x11, local copies, waits for them, and re-layouts  3.64 us

profile of v2, /device:TPU:1, one launch (start us, length us, event | category | flops | bytes accessed | tf_op | source)
XLA Modules:
  0.0 52.9 jit_solution(11677924882739097738)
XLA Ops:
  0.0 0.0 copy-start.3
  0.0 0.7 %copy-done.3 = s32[384]{0:T(512)S(1)} copy-done((s32[384]{0:T(512)S(1)}, s32[384]{0:T(512)}, u32[]{:S(2)}) %copy-start.3) | copy-done | bytes 1560
  0.7 0.0 copy-start.4
  0.7 0.7 %copy-done.4 = s32[384]{0:T(512)S(1)} copy-done((s32[384]{0:T(512)S(1)}, s32[384]{0:T(512)}, u32[]{:S(2)}) %copy-start.4) | copy-done | bytes 1560
  1.4 0.0 copy-start.1
  1.4 0.0 copy-start.2
  1.4 0.7 %copy-done.1 = s32[256]{0:T(256)S(1)} copy-done((s32[256]{0:T(256)S(1)}, s32[256]{0:T(256)}, u32[]{:S(2)}) %copy-start.1) | copy-done | bytes 1048
  2.0 0.0 copy-done.2
  2.0 0.0 copy-start
  2.0 1.0 %copy-done = bf16[256,1024]{1,0:T(8,128)(2,1)S(1)} copy-done((bf16[256,1024]{1,0:T(8,128)(2,1)S(1)}, bf16[256,1024]{1,0:T(8,128)(2,1)}, u32[]{:S(2)}) %copy-start) | copy-done | bytes 524312
  3.1 49.2 %band.1 = f32[2,128]{1,0:T(2,128)S(1)} custom-call(bf16[256,1024]{1,0:T(8,128)(2,1)S(1)} %copy-done, s32[1,256]{1,0:T(1,128)S(1)} %bitcast.4, s32[1,128]{1,0:T(1,128)S(1)} %bitcast.5, s32[1,384]{1,0:T(1,128)S(1)} %reshape.17.pl_ref, s32[1,384]{1,0:T(1,128)S(1)} %reshape.18.pr_ref), custom_call_target="tpu_custom_call" | custom-call | tf_op jit(solution)/shard_map/band/pallas_call | solution.py:323
  52.3 0.6 %copy.7 = f32[256]{0:T(256)} copy(f32[256]{0:T(256)S(1)} %bitcast.3) | data formatting | bytes 2048
  (2 shorter events, 0.0 us)
Async XLA Ops:
  0.0 0.7 %copy-start.3 = (s32[384]{0:T(512)S(1)}, s32[384]{0:T(512)}, u32[]{:S(2)}) copy-start(s32[384]{0:T(512)} %param.8) | copy-start | bytes 4612
  0.7 0.7 %copy-start.4 = (s32[384]{0:T(512)S(1)}, s32[384]{0:T(512)}, u32[]{:S(2)}) copy-start(s32[384]{0:T(512)} %param.9) | copy-start | bytes 4612
  1.4 0.7 %copy-start.1 = (s32[256]{0:T(256)S(1)}, s32[256]{0:T(256)}, u32[]{:S(2)}) copy-start(s32[256]{0:T(256)} %param.6) | copy-start | bytes 3076
  1.4 0.7 %copy-start.2 = (s32[128]{0:T(128)S(1)}, s32[128]{0:T(128)}, u32[]{:S(2)}) copy-start(s32[128]{0:T(128)} %param.7) | copy-start | bytes 1540
  2.0 1.0 %copy-start = (bf16[256,1024]{1,0:T(8,128)(2,1)S(1)}, bf16[256,1024]{1,0:T(8,128)(2,1)}, u32[]{:S(2)}) copy-start(bf16[256,1024]{1,0:T(8,128)(2,1)} %emb_ref.1) | copy-start | bytes 1572868

commit v3 on v1

v3 whole, which is shorter than its diff:
```python
import functools

import jax
import jax.numpy as jnp
from jax import lax
from jax.experimental import pallas as pl
from jax.experimental.pallas import tpu as pltpu
from jax.sharding import PartitionSpec as P

BLOCK = 128
LINES = 16
PARTS = 4
VISITORS = ((4, -1, 5, 3, -5), (4, -3, -1, 5, 3), (-4, -2, 5, -1, 2), (-1, -4, 3, -2, 2))
PASSED = ((1,), (-7, 1), (1, 4), (-3, 4))
NV = len(VISITORS[0])
NP = max(len(p) for p in PASSED)
ROUTE = (
    (0, 0, 0, 0, 1, 0, -1),
    (0, 0, 0, 1, -1, 0, -3),
    (0, 0, 0, 2, 0, -1, 4),
    (0, 1, 0, 0, 1, 0, -1),
    (0, 1, 0, 1, 0, -1, 4),
    (0, 1, 0, 3, -1, 0, 1),
    (0, 2, 0, 0, 0, -1, 4),
    (0, 2, 0, 0, 1, 0, -1),
    (0, 2, 0, 1, -1, 0, 1),
    (0, 2, 0, 3, 0, 1, -4),
    (0, 3, 0, 0, -1, 0, 1),
    (0, 3, 0, 0, 1, 0, 3),
    (0, 3, 0, 1, 0, -1, 4),
    (0, 3, 0, 1, 0, 1, -4),
    (1, 0, 0, 2, -1, 0, -3),
    (1, 0, 0, 3, 0, -1, 4),
    (1, 0, 0, 3, 1, 0, -1),
    (1, 1, 0, 0, 0, -1, 4),
    (1, 1, 0, 2, 1, 0, -1),
    (1, 2, 0, 0, 0, 1, -4),
    (1, 2, 0, 1, 1, 0, -1),
    (1, 2, 0, 2, -1, 0, 1),
    (1, 3, 0, 1, 1, 0, 3),
    (1, 3, 0, 2, 0, -1, 4),
    (1, 3, 0, 2, 0, 1, -4),
    (1, 3, 0, 3, -1, 0, 1),
    (1, 0, 0, 0, 0, -1, 4),
    (1, 0, 0, 2, 1, 0, -1),
    (1, 1, 0, 2, 0, -1, 4),
    (1, 1, 0, 3, 1, 0, -1),
    (1, 2, 0, 1, 0, 1, -4),
    (1, 2, 0, 2, 1, 0, -1),
    (1, 3, 0, 3, 0, 1, -4),
    (1, 0, 0, 1, 0, -1, 4),
    (1, 1, 0, 3, 0, -1, 4),
    (1, 2, 0, 2, 0, 1, -4),
    (1, 2, 0, 3, 1, 0, -1),
    (1, 3, 0, 0, 0, 1, -4),
    (2, 0, 3, 0, 0, 1, -1),
    (2, 1, 1, 1, 0, 1, -3),
    (2, 1, 4, 1, -1, 0, 5),
    (2, 2, 1, 0, 0, -1, 5),
    (2, 0, 1, 3, -1, 0, -2),
    (2, 2, -4, 3, -1, 0, -3),
    (2, 3, -4, 1, 1, 0, -1),
    (2, 3, -3, 1, -1, 0, -2),
    (2, 3, -1, 0, 0, -1, 3),
    (2, 0, 4, 2, 1, 0, 3),
    (2, 1, -1, 0, 1, 0, -2),
    (2, 3, 4, 1, -1, 0, 5),
    (2, 1, 1, 1, 0, -1, 5),
    (2, 2, -1, 0, 1, 0, -2),
    (2, 2, 4, 0, -1, 0, 5),
    (3, 1, 1, 2, 0, 1, -3),
    (3, 1, 4, 0, -1, 0, 5),
    (3, 2, 1, 3, 0, -1, 5),
    (3, 2, -4, 0, -1, 0, -3),
    (3, 3, -4, 2, 1, 0, -1),
    (3, 3, -1, 1, 0, -1, 3),
    (3, 0, 4, 3, 1, 0, 3),
    (3, 1, -1, 3, 1, 0, -2),
    (3, 3, -3, 2, -1, 0, -2),
    (3, 1, 1, 2, 0, -1, 5),
    (3, 2, -1, 2, 1, 0, -2),
    (3, 3, 4, 2, -1, 0, 5),
    (4, 0, -1, 0, 0, 1, -5),
    (4, 0, 5, 1, -1, 0, 2),
    (5, 0, -1, 1, 0, 1, -5),
    (5, 1, -3, 3, 0, 1, -7),
    (5, 1, 4, 2, -1, 0, 5),
    (5, 2, -2, 1, 0, -1, 2),
    (5, 3, -4, 3, 1, 0, -1),
    (5, 3, -1, 2, 0, -1, 3),
    (5, 0, 4, 0, 1, 0, 3),
    (5, 2, -2, 1, -1, 0, -1),
    (6, 0, 5, 0, -1, 0, 2),
    (7, 0, -1, 2, 0, 1, -5),
    (7, 0, -1, 2, 0, -1, 3),
    (7, 1, 4, 3, -1, 0, 5),
    (7, 2, -2, 0, 0, -1, 2),
    (7, 3, 2, 1, 0, 1, -2),
    (7, 1, 3, 2, 1, 0, 2),
    (7, 3, -1, 3, 0, -1, 3),
    (8, 1, -7, 3, 0, 1, 5),
    (8, 0, 5, 2, -1, 0, 2),
    (8, 2, 2, 1, -1, 0, 3),
    (9, 0, -1, 3, 0, 1, -5),
    (9, 0, -1, 3, 0, -1, 3),
    (9, 1, 3, 3, 1, 0, 2),
    (10, 0, 5, 3, -1, 0, 2),
    (10, 3, -2, 1, -1, 0, -1),
)
MESH = pl.DeviceIdType.MESH
F32 = jnp.float32
BF16 = jnp.bfloat16


def iota(shape, axis):
    return lax.broadcasted_iota(jnp.int32, shape, axis)


def dot_nt(a, b):
    return lax.dot_general(a, b, (((1,), (1,)), ((), ())), preferred_element_type=F32)


def dot_nn(a, b):
    return lax.dot_general(a, b, (((1,), (0,)), ((), ())), preferred_element_type=F32)


def onehot(mask):
    return jnp.where(mask, F32(1.0), F32(0.0)).astype(BF16)


def slot_of(c, offset):
    return (VISITORS[c] + PASSED[c]).index(offset)


def choose(x, values):
    value = jnp.int32(values[0])
    for c in range(1, 4):
        value = jnp.where(x == c, jnp.int32(values[c]), value)
    return value


def kernel(
    emb_in, lab_in, req_in, pl_in, pr_in, out_ref,
    emb_ref, lab_ref, req_ref, pl_ref, pr_ref, in_sem,
    line, vis, wout, win, pout, pin, lcol, elab, racc, cacc, rout, rin, cout, cin,
    z_send, z_recv, p_send, p_recv, v_send, v_recv, w_send, w_recv, q_send, q_recv,
    r_send, r_recv, c_send, c_recv,
):
    rows = emb_ref.shape[0]
    half = rows // 2
    piece = rows // PARTS
    me = lax.axis_index("dev")
    core = lax.rem(me, 2)
    z = lax.rem(me // 2, 4)
    ln = me // 8
    x = lax.rem(ln, 4)
    y = ln // 4

    def dev(dl, dz, dk):
        to_l = lax.rem(ln + dl + LINES, LINES)
        to_z = lax.rem(z + dz, 4)
        to_k = lax.rem(core + dk, 2)
        return to_l * 8 + to_z * 2 + to_k

    pairs = ((emb_in, emb_ref), (lab_in, lab_ref), (req_in, req_ref), (pl_in, pl_ref), (pr_in, pr_ref))
    fetch = [pltpu.make_async_copy(src, dst, in_sem.at[i]) for i, (src, dst) in enumerate(pairs)]
    for copy in fetch:
        copy.start()
    barrier = pltpu.get_barrier_semaphore()
    peers = [dev(0, s % 4, s // 4) for s in range(1, 8)] + [dev(j, 0, 0) for j in range(1, LINES)]
    for peer in peers:
        pl.semaphore_signal(barrier, inc=1, device_id=(peer,), device_id_type=MESH)

    def remote(src, dst, send, recv, to):
        return pltpu.make_async_remote_copy(
            src_ref=src, dst_ref=dst, send_sem=send, recv_sem=recv, device_id=(to,), device_id_type=MESH
        )

    cin[...] = jnp.full(cin.shape, -1.0, F32)
    racc[...] = jnp.full(racc.shape, -1.0, F32)
    cacc[...] = jnp.full(cacc.shape, -1.0, F32)

    fetch[0].wait()

    @pl.loop(0, rows // 64)
    def _(i):
        at = pl.ds(pl.multiple_of(i * 64, 64), 64)
        v = emb_ref[at, :].astype(F32)
        total = jnp.sum(v * v, axis=1, keepdims=True)
        line[0, at, :] = (v * lax.rsqrt(total + 1e-06)).astype(BF16)

    for copy in fetch[1:]:
        copy.wait()
    asked = req_ref[...].reshape(1, -1)
    firsts = pl_ref[...].reshape(1, -1)
    seconds = pr_ref[...].reshape(1, -1)
    expand = onehot((iota((256, 128), 0) // 2 == iota((256, 128), 1)) & (asked == iota((256, 128), 0) % 2))
    left = dot_nn(expand, onehot(iota((128, firsts.shape[1]), 0) == firsts)).astype(BF16)
    right = dot_nn(expand, onehot(iota((128, seconds.shape[1]), 0) == seconds)).astype(BF16)
    want = (dot_nt(left, right) + dot_nt(right, left)).astype(BF16)
    tags = lab_ref[...].reshape(1, -1).astype(F32)
    labels = jnp.concatenate(
        [jnp.broadcast_to(tags[:, h * BLOCK : (h + 1) * BLOCK], (8, BLOCK)) for h in range(2)], axis=0
    ).astype(BF16)
    group = iota((1, BLOCK), 1) // 16
    for j in range(LINES):
        offset = jnp.full((1, BLOCK), -1, jnp.int32)
        for m, d in enumerate((0,) + VISITORS[j % 4]):
            offset = jnp.where(group == m, ((j + d) % LINES) * 16 + iota((1, BLOCK), 1) % 16, offset)
        wout[j, 0:16, :] = dot_nn(want[16 * j : 16 * j + 16, :], onehot(iota((256, BLOCK), 0) == offset)).astype(BF16)
        wout[j, 16:32, :] = labels

    pl.semaphore_wait(barrier, len(peers))

    up_a = remote(line.at[0, 0:half], line.at[3, 0:half], z_send.at[0], z_recv.at[0], dev(0, 1, 0))
    dn_b = remote(line.at[0, half:rows], line.at[1, half:rows], z_send.at[1], z_recv.at[1], dev(0, 3, 0))
    up_b = remote(line.at[0, half:rows], line.at[3, half:rows], z_send.at[2], z_recv.at[2], dev(0, 1, 0))
    dn_a = remote(line.at[0, 0:half], line.at[1, 0:half], z_send.at[3], z_recv.at[3], dev(0, 3, 0))
    far_a = remote(line.at[3, 0:half], line.at[2, 0:half], z_send.at[4], z_recv.at[4], dev(0, 1, 0))
    far_b = remote(line.at[1, half:rows], line.at[2, half:rows], z_send.at[5], z_recv.at[5], dev(0, 3, 0))
    share = [
        remote(line.at[r], line.at[4 + r], p_send.at[r], p_recv.at[r], dev(0, 0, 1)) for r in (0, 1, 3)
    ]
    share.insert(2, None)
    far_share = [
        remote(line.at[2, at], line.at[6, at], p_send.at[i], p_recv.at[i], dev(0, 0, 1))
        for i, at in ((2, pl.ds(0, half)), (4, pl.ds(half, half)))
    ]

    waited = {c: set() for c in range(4)}

    def visit(n):
        _, c, held, part, dx, dy, becomes = ROUTE[n]
        at = pl.ds(part * piece, piece)
        src = line.at[0, at] if held == 0 else vis.at[slot_of(c, held), at]
        slot = slot_of((c + dx) % 4, becomes)
        to = (lax.rem(y + dy + 4, 4) * 4 + (c + dx) % 4) * 8 + z * 2 + core
        return remote(src, vis.at[slot, at], v_send.at[n], v_recv.at[slot, part], to)

    def arrive(c, offset, part):
        if (offset, part) not in waited[c]:
            waited[c].add((offset, part))
            at = pl.ds(part * piece, piece)
            slot = slot_of(c, offset)
            remote(
                line.at[0, at], vis.at[slot, at], v_send.at[0], v_recv.at[slot, part], dev(1, 0, 0)
            ).wait_recv()

    def spread(stage):
        for c in range(4):
            numbers = [n for n, e in enumerate(ROUTE) if e[0] == stage and e[1] == c]
            if numbers:

                @pl.when(x == c)
                def _():
                    for n in numbers:
                        if stage > 1:
                            arrive(c, ROUTE[n][2], ROUTE[n][3])
                        visit(n).start()

    def settle(m):
        for c in range(4):
            parts = [p for p in range(PARTS) if (VISITORS[c][m - 1], p) not in waited[c]]
            if parts:

                @pl.when(x == c)
                def _():
                    for p in parts:
                        arrive(c, VISITORS[c][m - 1], p)

    tell = [
        remote(
            wout.at[lax.rem(ln + j, LINES)], win.at[LINES - j], w_send.at[j], w_recv.at[LINES - j], dev(j, 0, 0)
        )
        for j in range(1, LINES)
    ]
    back = [(4 - s % 4) % 4 + 4 * (s // 4) for s in range(8)]
    pool = [
        remote(pout, pin.at[back[s]], q_send.at[s], q_recv.at[back[s]], dev(0, s % 4, s // 4)) for s in range(1, 8)
    ]

    up_a.start()
    dn_b.start()
    share[0].start()
    spread(0)

    for copy in tell:
        copy.start()
    spread(1)
    spread(2)
    total = wout[ln, 0:16, :].astype(F32)
    for copy in tell:
        copy.wait_recv()
    for j in range(1, LINES):
        total = total + win[j, 0:16, :].astype(F32)
    pout[0:16, :] = total.astype(BF16)
    pout[16:32, :] = labels
    for copy in pool:
        copy.start()
    up_b.start()
    dn_a.start()

    up_a.wait_recv()
    far_a.start()
    dn_b.wait_recv()
    far_b.start()
    spread(3)
    spread(4)
    spread(5)
    spread(6)

    for copy in pool:
        copy.wait_recv()
    for s in range(1, 8):
        total = total + pin[s, 0:16, :].astype(F32)
    total = total.astype(BF16)

    eye = iota((BLOCK, BLOCK), 0) == iota((BLOCK, BLOCK), 1)
    ones = jnp.full((BLOCK, BLOCK), 1.0, BF16)
    for s in range(8):
        both = (labels if s == 0 else pin[s, 16:32, :]).astype(F32)
        for h in range(2):
            diag = jnp.where(eye, jnp.broadcast_to(both[8 * h : 8 * h + 1, :], (BLOCK, BLOCK)), F32(0.0))
            lcol[2 * s + h] = dot_nn(diag.astype(BF16), ones)

    offsets = [jnp.int32(0)] + [choose(x, [VISITORS[c][m] for c in range(4)]) for m in range(NV)]
    for m in range(NV + 1):
        column = m * 16 + (z * 2 + core) * 2
        pick = onehot(iota((BLOCK, rows), 0) == column + iota((BLOCK, rows), 1) // BLOCK)
        listed = dot_nn(total, pick)
        theirs = (labels if m == 0 else win[lax.rem(offsets[m] + LINES, LINES), 16:32, :]).astype(F32)
        theirs = jnp.concatenate([theirs[0:1, :], theirs[8:9, :]], axis=1)
        elab[m] = jnp.where(listed > 0.5, theirs, F32(-1.0))

    def tile(m, s):
        rhs = line.at[0] if m == 0 else vis.at[m - 1]
        sims = dot_nt(line[s], rhs[...])
        base = (lax.rem(z + s % 4, 4) * 2 + lax.rem(core + s // 4, 2)) * 2
        cols = []
        for h in range(2):
            lc = lcol[2 * s + h]
            wanted = elab[m, pl.ds(base + h, 1), :]
            best = None
            parts = []
            for q in range(2):
                at = slice(q * BLOCK, (q + 1) * BLOCK)
                same = lc == wanted[:, at]
                if m == 0 and s == 0 and h == q:
                    same = same & jnp.logical_not(eye)
                val = jnp.where(same, sims[h * BLOCK : (h + 1) * BLOCK, at], F32(-1.0))
                best = val if best is None else jnp.maximum(best, val)
                parts.append(jnp.max(val.reshape(16, 8, BLOCK), axis=0))
            if m > 0:
                racc[2 * s + h] = jnp.maximum(racc[2 * s + h], best)
            cols.append(jnp.concatenate(parts, axis=1))
        cacc[m] = jnp.maximum(cacc[m], jnp.maximum(cols[0], cols[1]))

    def tiles(ms, slots):
        for m in ms:
            for s in slots:
                tile(m, s)

    give = []

    def column_out(m):
        top = jnp.max(cacc[m], axis=0, keepdims=True)
        cout[m, 0:1, :] = top[:, 0:BLOCK]
        cout[m, 1:2, :] = top[:, BLOCK:]
        if m > 0:
            at = lax.rem(offsets[m] + LINES, LINES)
            copy = remote(cout.at[m], cin.at[at], c_send.at[m - 1], c_recv.at[at], dev(offsets[m], 0, 0))
            copy.start()
            give.append(copy)

    lines_back = []

    def row_out(s):
        for h in range(2):
            rout[s, h : h + 1, :] = jnp.max(jnp.transpose(racc[2 * s + h]), axis=0, keepdims=True)
        if s > 0:
            copy = remote(rout.at[s], rin.at[back[s]], r_send.at[s], r_recv.at[back[s]], dev(0, s % 4, s // 4))
            copy.start()
            lines_back.append(copy)

    share[0].wait_recv()
    tiles([0], [0, 4])
    spread(7)
    up_b.wait_recv()
    share[3].start()
    dn_a.wait_recv()
    share[1].start()
    settle(1)
    tiles([1], [0, 4])
    spread(8)
    tiles([0], [1, 3])
    spread(9)
    tiles([1], [1, 3])
    spread(10)
    spread(11)
    spread(12)
    share[3].wait_recv()
    share[1].wait_recv()
    tiles([0, 1], [5, 7])
    settle(2)
    tiles([2], [0, 4, 1])
    far_a.wait_recv()
    far_share[0].start()
    far_b.wait_recv()
    far_share[1].start()
    tiles([2], [3, 5, 7])
    settle(3)
    tiles([3], [0, 4, 1, 3, 5, 7])
    tiles([0, 1, 2, 3], [2])
    settle(4)
    tiles([4], [0, 4, 1, 3, 5, 7, 2])
    for copy in far_share:
        copy.wait_recv()
    tiles([0, 1, 2, 3, 4], [6])
    for m in range(5):
        column_out(m)
    settle(5)
    for s in (6, 2, 5, 7, 1, 3, 4, 0):
        tile(5, s)
        row_out(s)
    column_out(5)

    result = jnp.maximum(rout[0], cout[0])
    for c in range(4):
        sources = [d for k in range(4) for d in VISITORS[k] if (k + d) % 4 == c]

        @pl.when(x == c)
        def _():
            for d in sources:
                at = d % LINES
                remote(cout.at[1], cin.at[at], c_send.at[0], c_recv.at[at], dev(1, 0, 0)).wait_recv()

    for copy in lines_back:
        copy.wait_recv()
    for j in range(1, LINES):
        result = jnp.maximum(result, cin[j])
    for s in range(1, 8):
        result = jnp.maximum(result, rin[s])
    out_ref[...] = result
    for copy in [up_a, up_b, dn_a, dn_b, far_a, far_b] + share[:2] + share[3:] + far_share + tell + pool + give + lines_back:
        copy.wait_send()
    for c in range(4):

        @pl.when(x == c)
        def _():
            for offset, part in [(d, p) for d in PASSED[c] for p in range(PARTS)]:
                if any((e[1] + e[4]) % 4 == c and e[6] == offset and e[3] == part for e in ROUTE):
                    arrive(c, offset, part)
            for n, entry in enumerate(ROUTE):
                if entry[1] == c:
                    visit(n).wait_send()


def local(embeddings, cluster_id, requests, pair_left, pair_right):
    rows, width = embeddings.shape
    dma = pltpu.SemaphoreType.DMA
    vmem = pltpu.VMEM
    scratch = [
        vmem((rows, width), BF16),
        vmem(cluster_id.shape, jnp.int32),
        vmem(requests.shape, jnp.int32),
        vmem(pair_left.shape, jnp.int32),
        vmem(pair_right.shape, jnp.int32),
        dma((5,)),
        vmem((8, rows, width), BF16),
        vmem((NV + NP, rows, width), BF16),
        vmem((LINES, 32, BLOCK), BF16),
        vmem((LINES, 32, BLOCK), BF16),
        vmem((32, BLOCK), BF16),
        vmem((8, 32, BLOCK), BF16),
        vmem((16, BLOCK, BLOCK), F32),
        vmem((NV + 1, 16, rows), F32),
        vmem((16, BLOCK, BLOCK), F32),
        vmem((NV + 1, 8, rows), F32),
        vmem((8, 2, BLOCK), F32),
        vmem((8, 2, BLOCK), F32),
        vmem((NV + 1, 2, BLOCK), F32),
        vmem((LINES, 2, BLOCK), F32),
    ]
    for sent, received in (
        ((6,), (6,)),
        ((5,), (5,)),
        ((len(ROUTE),), (NV + NP, PARTS)),
        ((LINES,), (LINES,)),
        ((8,), (8,)),
        ((8,), (8,)),
        ((NV,), (LINES,)),
    ):
        scratch += [dma(sent), dma(received)]
    best = pl.pallas_call(
        kernel,
        out_shape=jax.ShapeDtypeStruct((2, BLOCK), F32),
        in_specs=[pl.BlockSpec(memory_space=pl.ANY)] * 5,
        out_specs=pl.BlockSpec(memory_space=pltpu.VMEM),
        scratch_shapes=scratch,
        compiler_params=pltpu.CompilerParams(
            collective_id=0, has_side_effects=True, vmem_limit_bytes=67_000_000
        ),
        name="band",
    )(embeddings, cluster_id, requests, pair_left, pair_right)
    return best.reshape(-1)


def solution(mesh):
    in_specs = (P("dev", None), P("dev"), P("dev"), P("dev"), P("dev"))
    out_specs = P("dev")
    return jax.shard_map(local, mesh=mesh, in_specs=in_specs, out_specs=out_specs, check_vma=False)
```

time: 79.6 us -> 47.7 us (0.60)
  Pallas kernels: 75.8 us -> 46.4 us
  local copies, waits for them, and re-layouts: 3.65 us -> 1.22 us
    pallas_call x1, Pallas kernels: 75.8 us -> 46.4 us  [local(): pl.pallas_call(kernel, out_shape=jax.ShapeDtypeStruct((2, BLOCK), F32), i...]
    unnamed x11 -> x3, local copies, waits for them, and re-layouts: 3.64 us -> 1.22 us
where the time goes in v3:
time: 47.7 us; the launch traced here: 47.6 us
  Pallas kernels  46.4 us (97%)
  local copies, waits for them, and re-layouts  1.22 us (3%)
    pallas_call x1, Pallas kernels, local(): pl.pallas_call(kernel, out_shape=jax.ShapeDtypeStruct((2, BLOCK), F32), i...  46.4 us
    unnamed x3, local copies, waits for them, and re-layouts  1.22 us

profile of v3, /device:TPU:1, one launch (start us, length us, event | category | flops | bytes accessed | tf_op | source)
XLA Modules:
  0.0 47.6 jit_solution(4706972726447641599)
XLA Ops:
  0.0 46.4 %band.1 = f32[2,128]{1,0:T(2,128)} custom-call(bf16[256,1024]{1,0:T(8,128)(2,1)} %emb_in.1, s32[256]{0:T(256)} %lab_in.1, s32[128]{0:T(128)} %req_in.1, s32[384]{0:T(512)} %pl_in.1, s32[384]{0:T(512)} %pr_in.1), custom_call_target="tpu_custom_call" | custom-call | tf_op jit(solution)/shard_map/band/pallas_call | solution.py:494
  46.4 0.0 copy-start
  46.4 0.7 %copy-done = f32[2,128]{1,0:T(2,128)S(1)} copy-done((f32[2,128]{1,0:T(2,128)S(1)}, f32[2,128]{1,0:T(2,128)}, u32[]{:S(2)}) %copy-start) | copy-done | bytes 1048
  47.0 0.6 %copy.7 = f32[256]{0:T(256)} copy(f32[256]{0:T(256)S(1)} %bitcast.1) | data formatting | bytes 2048
Async XLA Ops:
  46.4 0.7 %copy-start = (f32[2,128]{1,0:T(2,128)S(1)}, f32[2,128]{1,0:T(2,128)}, u32[]{:S(2)}) copy-start(f32[2,128]{1,0:T(2,128)} %band.1) | copy-start | bytes 3076

commit v4 on v3

--- a/solution.py
+++ b/solution.py
@@ -1,5 +1,3 @@
-import functools
-
 import jax
 import jax.numpy as jnp
 from jax import lax
@@ -10,102 +8,107 @@
 BLOCK = 128
 LINES = 16
 PARTS = 4
-VISITORS = ((4, -1, 5, 3, -5), (4, -3, -1, 5, 3), (-4, -2, 5, -1, 2), (-1, -4, 3, -2, 2))
-PASSED = ((1,), (-7, 1), (1, 4), (-3, 4))
+VISITORS = ((4, -1, 3, -5, -2), (-1, 4, -3, -5, 3), (-1, 4, -5, -2, 5), (-4, 3, -2, -1, 2))
+PASSED = ((-4, 1, 5), (1,), (-4, 1), (-8, -3, 4))
 NV = len(VISITORS[0])
 NP = max(len(p) for p in PASSED)
 ROUTE = (
+    (0, 0, 0, 0, -1, 0, -3),
+    (0, 0, 0, 0, 0, 1, -4),
     (0, 0, 0, 0, 1, 0, -1),
-    (0, 0, 0, 1, -1, 0, -3),
     (0, 0, 0, 2, 0, -1, 4),
     (0, 1, 0, 0, 1, 0, -1),
-    (0, 1, 0, 1, 0, -1, 4),
-    (0, 1, 0, 3, -1, 0, 1),
+    (0, 1, 0, 1, -1, 0, 1),
+    (0, 1, 0, 3, 0, -1, 4),
+    (0, 2, 0, 0, -1, 0, 1),
     (0, 2, 0, 0, 0, -1, 4),
-    (0, 2, 0, 0, 1, 0, -1),
-    (0, 2, 0, 1, -1, 0, 1),
-    (0, 2, 0, 3, 0, 1, -4),
-    (0, 3, 0, 0, -1, 0, 1),
+    (0, 2, 0, 1, 0, 1, -4),
+    (0, 2, 0, 1, 1, 0, -1),
+    (0, 3, 0, 0, 0, -1, 4),
     (0, 3, 0, 0, 1, 0, 3),
-    (0, 3, 0, 1, 0, -1, 4),
+    (0, 3, 0, 1, -1, 0, 1),
     (0, 3, 0, 1, 0, 1, -4),
-    (1, 0, 0, 2, -1, 0, -3),
+    (1, 0, 0, 0, 0, -1, 4),
+    (1, 0, 0, 1, 1, 0, -1),
+    (1, 0, 0, 3, -1, 0, -3),
+    (1, 0, 0, 3, 0, 1, -4),
+    (1, 1, 0, 0, 0, -1, 4),
+    (1, 1, 0, 1, 1, 0, -1),
+    (1, 1, 0, 2, -1, 0, 1),
+    (1, 2, 0, 2, 0, -1, 4),
+    (1, 2, 0, 2, 0, 1, -4),
+    (1, 2, 0, 3, -1, 0, 1),
+    (1, 2, 0, 3, 1, 0, -1),
+    (1, 3, 0, 2, -1, 0, 1),
+    (1, 3, 0, 2, 0, 1, -4),
+    (1, 3, 0, 3, 0, -1, 4),
+    (1, 3, 0, 3, 1, 0, 3),
+    (1, 0, 0, 1, 0, -1, 4),
+    (1, 0, 0, 2, 1, 0, -1),
+    (1, 1, 0, 1, 0, -1, 4),
+    (1, 1, 0, 2, 1, 0, -1),
+    (1, 2, 0, 1, 0, -1, 4),
+    (1, 3, 0, 1, 1, 0, 3),
+    (1, 3, 0, 3, 0, 1, -4),
     (1, 0, 0, 3, 0, -1, 4),
     (1, 0, 0, 3, 1, 0, -1),
-    (1, 1, 0, 0, 0, -1, 4),
-    (1, 1, 0, 2, 1, 0, -1),
-    (1, 2, 0, 0, 0, 1, -4),
-    (1, 2, 0, 1, 1, 0, -1),
-    (1, 2, 0, 2, -1, 0, 1),
-    (1, 3, 0, 1, 1, 0, 3),
-    (1, 3, 0, 2, 0, -1, 4),
-    (1, 3, 0, 2, 0, 1, -4),
-    (1, 3, 0, 3, -1, 0, 1),
-    (1, 0, 0, 0, 0, -1, 4),
-    (1, 0, 0, 2, 1, 0, -1),
     (1, 1, 0, 2, 0, -1, 4),
     (1, 1, 0, 3, 1, 0, -1),
-    (1, 2, 0, 1, 0, 1, -4),
-    (1, 2, 0, 2, 1, 0, -1),
-    (1, 3, 0, 3, 0, 1, -4),
-    (1, 0, 0, 1, 0, -1, 4),
-    (1, 1, 0, 3, 0, -1, 4),
-    (1, 2, 0, 2, 0, 1, -4),
-    (1, 2, 0, 3, 1, 0, -1),
-    (1, 3, 0, 0, 0, 1, -4),
+    (1, 2, 0, 3, 0, -1, 4),
+    (2, 1, 1, 0, 0, 1, -3),
+    (2, 0, 1, 1, -1, 0, -2),
     (2, 0, 3, 0, 0, 1, -1),
-    (2, 1, 1, 1, 0, 1, -3),
-    (2, 1, 4, 1, -1, 0, 5),
-    (2, 2, 1, 0, 0, -1, 5),
-    (2, 0, 1, 3, -1, 0, -2),
-    (2, 2, -4, 3, -1, 0, -3),
+    (2, 1, 4, 3, -1, 0, 5),
+    (2, 2, -4, 1, -1, 0, -3),
+    (2, 2, -1, 0, 0, 1, -5),
+    (2, 2, -1, 0, 1, 0, -2),
+    (2, 3, -3, 0, -1, 0, -2),
+    (2, 3, -1, 1, 0, -1, 3),
+    (2, 2, 4, 0, 1, 0, 3),
     (2, 3, -4, 1, 1, 0, -1),
-    (2, 3, -3, 1, -1, 0, -2),
-    (2, 3, -1, 0, 0, -1, 3),
+    (2, 3, 4, 0, -1, 0, 5),
+    (2, 0, -4, 0, 1, 0, -5),
+    (2, 1, -1, 0, 0, -1, 3),
+    (2, 2, 1, 1, 0, -1, 5),
     (2, 0, 4, 2, 1, 0, 3),
-    (2, 1, -1, 0, 1, 0, -2),
-    (2, 3, 4, 1, -1, 0, 5),
-    (2, 1, 1, 1, 0, -1, 5),
-    (2, 2, -1, 0, 1, 0, -2),
-    (2, 2, 4, 0, -1, 0, 5),
-    (3, 1, 1, 2, 0, 1, -3),
-    (3, 1, 4, 0, -1, 0, 5),
-    (3, 2, 1, 3, 0, -1, 5),
-    (3, 2, -4, 0, -1, 0, -3),
+    (3, 1, 1, 3, 0, 1, -3),
+    (3, 1, -1, 1, 0, 1, -5),
+    (3, 0, 1, 2, -1, 0, -2),
+    (3, 0, 3, 3, 0, 1, -1),
+    (3, 2, -4, 2, -1, 0, -3),
+    (3, 2, -1, 1, 0, 1, -5),
+    (3, 3, -4, 2, 0, 1, -8),
+    (3, 3, -1, 3, 0, -1, 3),
+    (3, 1, -1, 1, 1, 0, -2),
+    (3, 2, 4, 2, 1, 0, 3),
     (3, 3, -4, 2, 1, 0, -1),
-    (3, 3, -1, 1, 0, -1, 3),
-    (3, 0, 4, 3, 1, 0, 3),
-    (3, 1, -1, 3, 1, 0, -2),
-    (3, 3, -3, 2, -1, 0, -2),
-    (3, 1, 1, 2, 0, -1, 5),
-    (3, 2, -1, 2, 1, 0, -2),
-    (3, 3, 4, 2, -1, 0, 5),
-    (4, 0, -1, 0, 0, 1, -5),
-    (4, 0, 5, 1, -1, 0, 2),
-    (5, 0, -1, 1, 0, 1, -5),
-    (5, 1, -3, 3, 0, 1, -7),
-    (5, 1, 4, 2, -1, 0, 5),
-    (5, 2, -2, 1, 0, -1, 2),
-    (5, 3, -4, 3, 1, 0, -1),
-    (5, 3, -1, 2, 0, -1, 3),
-    (5, 0, 4, 0, 1, 0, 3),
-    (5, 2, -2, 1, -1, 0, -1),
-    (6, 0, 5, 0, -1, 0, 2),
-    (7, 0, -1, 2, 0, 1, -5),
-    (7, 0, -1, 2, 0, -1, 3),
-    (7, 1, 4, 3, -1, 0, 5),
-    (7, 2, -2, 0, 0, -1, 2),
-    (7, 3, 2, 1, 0, 1, -2),
-    (7, 1, 3, 2, 1, 0, 2),
-    (7, 3, -1, 3, 0, -1, 3),
-    (8, 1, -7, 3, 0, 1, 5),
-    (8, 0, 5, 2, -1, 0, 2),
-    (8, 2, 2, 1, -1, 0, 3),
-    (9, 0, -1, 3, 0, 1, -5),
-    (9, 0, -1, 3, 0, -1, 3),
-    (9, 1, 3, 3, 1, 0, 2),
-    (10, 0, 5, 3, -1, 0, 2),
-    (10, 3, -2, 1, -1, 0, -1),
+    (3, 3, -3, 3, -1, 0, -2),
+    (3, 1, -1, 1, 0, -1, 3),
+    (3, 2, 1, 2, 0, -1, 5),
+    (3, 3, 4, 3, -1, 0, 5),
+    (3, 0, -4, 3, 1, 0, -5),
+    (4, 1, -3, 0, -1, 0, -2),
+    (5, 1, -1, 2, 0, 1, -5),
+    (5, 0, -1, 0, -1, 0, -4),
+    (5, 0, -1, 0, 0, 1, -5),
+    (5, 1, -3, 1, -1, 0, -2),
+    (5, 2, -1, 2, 0, 1, -5),
+    (5, 3, -2, 0, 0, -1, 2),
+    (5, 0, 5, 3, -1, 0, 2),
+    (5, 1, -1, 2, 1, 0, -2),
+    (5, 3, -2, 1, 0, -1, 2),
+    (6, 1, -3, 3, -1, 0, -2),
+    (7, 3, 3, 0, 0, 1, -1),
+    (7, 0, -1, 1, 0, 1, -5),
+    (7, 1, -3, 2, -1, 0, -2),
+    (7, 2, -1, 3, 0, 1, -5),
+    (7, 2, -1, 3, 1, 0, -2),
+    (7, 3, -8, 2, 1, 0, -5),
+    (7, 0, -1, 3, 0, 1, -5),
+    (7, 1, -1, 3, 0, -1, 3),
+    (7, 3, -2, 2, 0, -1, 2),
+    (9, 0, -1, 2, 0, -1, 3),
+    (9, 3, 3, 2, 0, 1, -1),
 )
 MESH = pl.DeviceIdType.MESH
 F32 = jnp.float32
@@ -350,7 +353,7 @@
                 val = jnp.where(same, sims[h * BLOCK : (h + 1) * BLOCK, at], F32(-1.0))
                 best = val if best is None else jnp.maximum(best, val)
                 parts.append(jnp.max(val.reshape(16, 8, BLOCK), axis=0))
-            if m > 0:
+            if m > 0 or s in (1, 5):
                 racc[2 * s + h] = jnp.maximum(racc[2 * s + h], best)
             cols.append(jnp.concatenate(parts, axis=1))
         cacc[m] = jnp.maximum(cacc[m], jnp.maximum(cols[0], cols[1]))
@@ -392,7 +395,7 @@
     settle(1)
     tiles([1], [0, 4])
     spread(8)
-    tiles([0], [1, 3])
+    tiles([0], [1])
     spread(9)
     tiles([1], [1, 3])
     spread(10)
@@ -400,7 +403,8 @@
     spread(12)
     share[3].wait_recv()
     share[1].wait_recv()
-    tiles([0, 1], [5, 7])
+    tiles([0], [5])
+    tiles([1], [5, 7])
     settle(2)
     tiles([2], [0, 4, 1])
     far_a.wait_recv()
@@ -411,18 +415,22 @@
     settle(3)
     tiles([3], [0, 4, 1, 3, 5, 7])
     tiles([0, 1, 2, 3], [2])
-    settle(4)
-    tiles([4], [0, 4, 1, 3, 5, 7, 2])
     for copy in far_share:
         copy.wait_recv()
-    tiles([0, 1, 2, 3, 4], [6])
-    for m in range(5):
+    tiles([0, 1, 2, 3], [6])
+    for m in range(4):
         column_out(m)
+    settle(4)
+    tiles([4], [6, 2, 0, 4, 1, 3, 5, 7])
+    column_out(4)
     settle(5)
-    for s in (6, 2, 5, 7, 1, 3, 4, 0):
+    for s in (6, 2):
         tile(5, s)
         row_out(s)
+    tiles([5], [5, 7, 1, 3, 4, 0])
     column_out(5)
+    for s in (5, 7, 1, 3, 4, 0):
+        row_out(s)
 
     result = jnp.maximum(rout[0], cout[0])
     for c in range(4):

time: 47.7 us -> 44.1 us (0.925)
  Pallas kernels: 46.4 us -> 42.8 us
    pallas_call x1, Pallas kernels: 46.4 us -> 42.8 us  [local(): pl.pallas_call(kernel, out_shape=jax.ShapeDtypeStruct((2, BLOCK), F32), i...]
where the time goes in v4:
time: 44.1 us; the launch traced here: 44 us
  Pallas kernels  42.8 us (97%)
  local copies, waits for them, and re-layouts  1.22 us (3%)
    pallas_call x1, Pallas kernels, local(): pl.pallas_call(kernel, out_shape=jax.ShapeDtypeStruct((2, BLOCK), F32), i...  42.8 us
    unnamed x3, local copies, waits for them, and re-layouts  1.22 us

profile of v4, /device:TPU:1, one launch (start us, length us, event | category | flops | bytes accessed | tf_op | source)
XLA Modules:
  0.0 44.0 jit_solution(9770896728033958612)
XLA Ops:
  0.0 42.8 %band.1 = f32[2,128]{1,0:T(2,128)} custom-call(bf16[256,1024]{1,0:T(8,128)(2,1)} %emb_in.1, s32[256]{0:T(256)} %lab_in.1, s32[128]{0:T(128)} %req_in.1, s32[384]{0:T(512)} %pl_in.1, s32[384]{0:T(512)} %pr_in.1), custom_call_target="tpu_custom_call" | custom-call | tf_op jit(solution)/shard_map/band/pallas_call | solution.py:502
  42.8 0.0 copy-start
  42.8 0.7 %copy-done = f32[2,128]{1,0:T(2,128)S(1)} copy-done((f32[2,128]{1,0:T(2,128)S(1)}, f32[2,128]{1,0:T(2,128)}, u32[]{:S(2)}) %copy-start) | copy-done | bytes 1048
  43.4 0.6 %copy.7 = f32[256]{0:T(256)} copy(f32[256]{0:T(256)S(1)} %bitcast.1) | data formatting | bytes 2048
Async XLA Ops:
  42.8 0.7 %copy-start = (f32[2,128]{1,0:T(2,128)S(1)}, f32[2,128]{1,0:T(2,128)}, u32[]{:S(2)}) copy-start(f32[2,128]{1,0:T(2,128)} %band.1) | copy-start | bytes 3076

commit v5 on v4

--- a/solution.py
+++ b/solution.py
@@ -284,11 +284,11 @@
 
     up_a.start()
     dn_b.start()
+    for copy in tell:
+        copy.start()
     share[0].start()
     spread(0)
 
-    for copy in tell:
-        copy.start()
     spread(1)
     spread(2)
     total = wout[ln, 0:16, :].astype(F32)
@@ -398,13 +398,13 @@
     tiles([0], [1])
     spread(9)
     tiles([1], [1, 3])
-    spread(10)
-    spread(11)
-    spread(12)
     share[3].wait_recv()
     share[1].wait_recv()
     tiles([0], [5])
     tiles([1], [5, 7])
+    spread(10)
+    spread(11)
+    spread(12)
     settle(2)
     tiles([2], [0, 4, 1])
     far_a.wait_recv()

time: 44.1 us -> 43.8 us (level)
  no operation moved by 1% of the time
where the time goes in v5:
time: 43.8 us; the launch traced here: 43.6 us
  Pallas kernels  42.4 us (97%)
  local copies, waits for them, and re-layouts  1.22 us (3%)
    pallas_call x1, Pallas kernels, local(): pl.pallas_call(kernel, out_shape=jax.ShapeDtypeStruct((2, BLOCK), F32), i...  42.4 us
    unnamed x3, local copies, waits for them, and re-layouts  1.22 us

profile of v5, /device:TPU:1, one launch (start us, length us, event | category | flops | bytes accessed | tf_op | source)
XLA Modules:
  0.0 43.6 jit_solution(9518495125689008008)
XLA Ops:
  0.0 42.4 %band.1 = f32[2,128]{1,0:T(2,128)} custom-call(bf16[256,1024]{1,0:T(8,128)(2,1)} %emb_in.1, s32[256]{0:T(256)} %lab_in.1, s32[128]{0:T(128)} %req_in.1, s32[384]{0:T(512)} %pl_in.1, s32[384]{0:T(512)} %pr_in.1), custom_call_target="tpu_custom_call" | custom-call | tf_op jit(solution)/shard_map/band/pallas_call | solution.py:502
  42.4 0.0 copy-start
  42.4 0.7 %copy-done = f32[2,128]{1,0:T(2,128)S(1)} copy-done((f32[2,128]{1,0:T(2,128)S(1)}, f32[2,128]{1,0:T(2,128)}, u32[]{:S(2)}) %copy-start) | copy-done | bytes 1048
  43.1 0.6 %copy.7 = f32[256]{0:T(256)} copy(f32[256]{0:T(256)S(1)} %bitcast.1) | data formatting | bytes 2048
Async XLA Ops:
  42.4 0.7 %copy-start = (f32[2,128]{1,0:T(2,128)S(1)}, f32[2,128]{1,0:T(2,128)}, u32[]{:S(2)}) copy-start(f32[2,128]{1,0:T(2,128)} %band.1) | copy-start | bytes 3076

commit v6 on v5

--- a/solution.py
+++ b/solution.py
@@ -8,107 +8,106 @@
 BLOCK = 128
 LINES = 16
 PARTS = 4
-VISITORS = ((4, -1, 3, -5, -2), (-1, 4, -3, -5, 3), (-1, 4, -5, -2, 5), (-4, 3, -2, -1, 2))
-PASSED = ((-4, 1, 5), (1,), (-4, 1), (-8, -3, 4))
+VISITORS = ((4, -1, 5, -5, -2), (4, -3, -1, 3, 2), (-1, 4, 5, -5, -2), (-3, -4, 3, -1, 2))
+PASSED = ((1, 3), (1,), (-4, 1), (-8, -5, -2, 4))
 NV = len(VISITORS[0])
 NP = max(len(p) for p in PASSED)
 ROUTE = (
-    (0, 0, 0, 0, -1, 0, -3),
-    (0, 0, 0, 0, 0, 1, -4),
     (0, 0, 0, 0, 1, 0, -1),
     (0, 0, 0, 2, 0, -1, 4),
-    (0, 1, 0, 0, 1, 0, -1),
-    (0, 1, 0, 1, -1, 0, 1),
-    (0, 1, 0, 3, 0, -1, 4),
+    (0, 0, 0, 3, -1, 0, -3),
+    (0, 1, 0, 0, 0, -1, 4),
+    (0, 1, 0, 2, 1, 0, -1),
+    (0, 1, 0, 3, -1, 0, 1),
     (0, 2, 0, 0, -1, 0, 1),
-    (0, 2, 0, 0, 0, -1, 4),
-    (0, 2, 0, 1, 0, 1, -4),
     (0, 2, 0, 1, 1, 0, -1),
+    (0, 2, 0, 3, 0, -1, 4),
+    (0, 2, 0, 3, 0, 1, -4),
     (0, 3, 0, 0, 0, -1, 4),
-    (0, 3, 0, 0, 1, 0, 3),
     (0, 3, 0, 1, -1, 0, 1),
     (0, 3, 0, 1, 0, 1, -4),
-    (1, 0, 0, 0, 0, -1, 4),
+    (0, 3, 0, 3, 1, 0, 3),
+    (1, 0, 0, 0, -1, 0, -3),
     (1, 0, 0, 1, 1, 0, -1),
-    (1, 0, 0, 3, -1, 0, -3),
-    (1, 0, 0, 3, 0, 1, -4),
-    (1, 1, 0, 0, 0, -1, 4),
-    (1, 1, 0, 1, 1, 0, -1),
-    (1, 1, 0, 2, -1, 0, 1),
-    (1, 2, 0, 2, 0, -1, 4),
+    (1, 0, 0, 3, 0, -1, 4),
+    (1, 1, 0, 0, 1, 0, -1),
+    (1, 1, 0, 1, 0, -1, 4),
+    (1, 2, 0, 0, 0, -1, 4),
+    (1, 2, 0, 1, -1, 0, 1),
     (1, 2, 0, 2, 0, 1, -4),
-    (1, 2, 0, 3, -1, 0, 1),
-    (1, 2, 0, 3, 1, 0, -1),
+    (1, 2, 0, 2, 1, 0, -1),
+    (1, 3, 0, 0, 1, 0, 3),
     (1, 3, 0, 2, -1, 0, 1),
     (1, 3, 0, 2, 0, 1, -4),
-    (1, 3, 0, 3, 0, -1, 4),
-    (1, 3, 0, 3, 1, 0, 3),
+    (1, 0, 0, 0, 0, -1, 4),
+    (1, 0, 0, 1, -1, 0, -3),
+    (1, 1, 0, 1, 1, 0, -1),
+    (1, 1, 0, 2, 0, -1, 4),
+    (1, 2, 0, 0, 1, 0, -1),
+    (1, 2, 0, 1, 0, -1, 4),
+    (1, 3, 0, 3, -1, 0, 1),
+    (1, 3, 0, 3, 0, 1, -4),
     (1, 0, 0, 1, 0, -1, 4),
-    (1, 0, 0, 2, 1, 0, -1),
-    (1, 1, 0, 1, 0, -1, 4),
-    (1, 1, 0, 2, 1, 0, -1),
-    (1, 2, 0, 1, 0, -1, 4),
-    (1, 3, 0, 1, 1, 0, 3),
-    (1, 3, 0, 3, 0, 1, -4),
-    (1, 0, 0, 3, 0, -1, 4),
-    (1, 0, 0, 3, 1, 0, -1),
-    (1, 1, 0, 2, 0, -1, 4),
+    (1, 0, 0, 2, -1, 0, -3),
+    (1, 1, 0, 3, 0, -1, 4),
     (1, 1, 0, 3, 1, 0, -1),
-    (1, 2, 0, 3, 0, -1, 4),
+    (2, 0, 3, 3, 0, 1, -1),
     (2, 1, 1, 0, 0, 1, -3),
-    (2, 0, 1, 1, -1, 0, -2),
-    (2, 0, 3, 0, 0, 1, -1),
-    (2, 1, 4, 3, -1, 0, 5),
-    (2, 2, -4, 1, -1, 0, -3),
-    (2, 2, -1, 0, 0, 1, -5),
-    (2, 2, -1, 0, 1, 0, -2),
-    (2, 3, -3, 0, -1, 0, -2),
+    (2, 1, 4, 0, -1, 0, 5),
+    (2, 3, 4, 0, 0, -1, -8),
+    (2, 0, 4, 2, 1, 0, 3),
+    (2, 2, -4, 3, -1, 0, -3),
+    (2, 3, -4, 1, 1, 0, -1),
+    (2, 2, -1, 2, 1, 0, -2),
+    (2, 2, 1, 1, -1, 0, 2),
+    (2, 2, 1, 1, 0, -1, 5),
     (2, 3, -1, 1, 0, -1, 3),
-    (2, 2, 4, 0, 1, 0, 3),
-    (2, 3, -4, 1, 1, 0, -1),
+    (2, 3, -1, 1, 0, 1, -5),
     (2, 3, 4, 0, -1, 0, 5),
-    (2, 0, -4, 0, 1, 0, -5),
+    (2, 0, 1, 3, 0, -1, 5),
     (2, 1, -1, 0, 0, -1, 3),
-    (2, 2, 1, 1, 0, -1, 5),
-    (2, 0, 4, 2, 1, 0, 3),
-    (3, 1, 1, 3, 0, 1, -3),
-    (3, 1, -1, 1, 0, 1, -5),
-    (3, 0, 1, 2, -1, 0, -2),
-    (3, 0, 3, 3, 0, 1, -1),
+    (2, 1, -1, 0, 1, 0, -2),
+    (2, 2, -1, 2, 0, 1, -5),
+    (2, 2, 4, 3, 1, 0, 3),
+    (2, 3, -3, 3, -1, 0, -2),
+    (2, 0, 3, 3, 1, 0, 2),
+    (3, 0, 3, 0, 0, 1, -1),
+    (3, 1, 1, 1, 0, 1, -3),
+    (3, 1, 4, 1, -1, 0, 5),
+    (3, 2, -1, 0, 0, 1, -5),
+    (3, 3, -1, 2, 0, -1, 3),
+    (3, 0, 4, 3, 1, 0, 3),
+    (3, 3, -4, 2, 1, 0, -1),
+    (3, 0, 3, 0, 1, 0, 2),
     (3, 2, -4, 2, -1, 0, -3),
-    (3, 2, -1, 1, 0, 1, -5),
-    (3, 3, -4, 2, 0, 1, -8),
-    (3, 3, -1, 3, 0, -1, 3),
+    (3, 2, 1, 2, 0, -1, 5),
+    (3, 3, -1, 2, 0, 1, -5),
+    (3, 1, -1, 1, 0, -1, 3),
     (3, 1, -1, 1, 1, 0, -2),
-    (3, 2, 4, 2, 1, 0, 3),
-    (3, 3, -4, 2, 1, 0, -1),
-    (3, 3, -3, 3, -1, 0, -2),
-    (3, 1, -1, 1, 0, -1, 3),
-    (3, 2, 1, 2, 0, -1, 5),
-    (3, 3, 4, 3, -1, 0, 5),
-    (3, 0, -4, 3, 1, 0, -5),
+    (3, 2, 1, 2, -1, 0, 2),
+    (3, 2, 4, 0, 1, 0, 3),
+    (4, 0, -1, 3, 0, 1, -5),
+    (4, 0, 5, 0, -1, 0, 2),
     (4, 1, -3, 0, -1, 0, -2),
-    (5, 1, -1, 2, 0, 1, -5),
-    (5, 0, -1, 0, -1, 0, -4),
-    (5, 0, -1, 0, 0, 1, -5),
-    (5, 1, -3, 1, -1, 0, -2),
-    (5, 2, -1, 2, 0, 1, -5),
-    (5, 3, -2, 0, 0, -1, 2),
-    (5, 0, 5, 3, -1, 0, 2),
-    (5, 1, -1, 2, 1, 0, -2),
-    (5, 3, -2, 1, 0, -1, 2),
-    (6, 1, -3, 3, -1, 0, -2),
-    (7, 3, 3, 0, 0, 1, -1),
-    (7, 0, -1, 1, 0, 1, -5),
-    (7, 1, -3, 2, -1, 0, -2),
+    (4, 3, -8, 0, 0, -1, -4),
+    (4, 3, -8, 0, 1, 0, -5),
+    (5, 0, -1, 1, 0, 1, -5),
+    (5, 1, 3, 2, 0, 1, -1),
+    (5, 1, 4, 2, -1, 0, 5),
+    (5, 2, -1, 1, 0, 1, -5),
+    (5, 1, -3, 3, -1, 0, -2),
+    (5, 2, 1, 3, 0, -1, 5),
+    (6, 0, 5, 1, -1, 0, 2),
+    (6, 3, 3, 2, -1, 0, 4),
+    (7, 0, -1, 2, 0, 1, -5),
+    (7, 1, 3, 3, 0, 1, -1),
     (7, 2, -1, 3, 0, 1, -5),
-    (7, 2, -1, 3, 1, 0, -2),
-    (7, 3, -8, 2, 1, 0, -5),
-    (7, 0, -1, 3, 0, 1, -5),
-    (7, 1, -1, 3, 0, -1, 3),
+    (7, 3, -5, 1, 1, 0, -2),
     (7, 3, -2, 2, 0, -1, 2),
-    (9, 0, -1, 2, 0, -1, 3),
-    (9, 3, 3, 2, 0, 1, -1),
+    (8, 1, -1, 2, 1, 0, -2),
+    (9, 3, 3, 3, 0, 1, -1),
+    (9, 0, 5, 3, -1, 0, 2),
+    (9, 3, -5, 2, 1, 0, -2),
 )
 MESH = pl.DeviceIdType.MESH
 F32 = jnp.float32
@@ -406,15 +405,16 @@
     spread(11)
     spread(12)
     settle(2)
-    tiles([2], [0, 4, 1])
+    tiles([2], [0, 4])
     far_a.wait_recv()
     far_share[0].start()
     far_b.wait_recv()
     far_share[1].start()
-    tiles([2], [3, 5, 7])
+    tiles([2], [1, 3, 5, 7])
+    tiles([0, 1, 2], [2])
     settle(3)
     tiles([3], [0, 4, 1, 3, 5, 7])
-    tiles([0, 1, 2, 3], [2])
+    tiles([3], [2])
     for copy in far_share:
         copy.wait_recv()
     tiles([0, 1, 2, 3], [6])

time: 43.8 us -> 43.6 us (level)
  the two profiles are of different devices: /device:TPU:1 before, /device:TPU:3 now
where the time goes in v6:
time: 43.6 us; the launch traced here: 43.5 us
  Pallas kernels  42.3 us (97%)
  local copies, waits for them, and re-layouts  1.22 us (3%)
    pallas_call x1, Pallas kernels, local(): pl.pallas_call(kernel, out_shape=jax.ShapeDtypeStruct((2, BLOCK), F32), i...  42.3 us
    unnamed x3, local copies, waits for them, and re-layouts  1.22 us

profile of v6, /device:TPU:3, one launch (start us, length us, event | category | flops | bytes accessed | tf_op | source)
XLA Modules:
  0.0 43.5 jit_solution(6537474415247040302)
XLA Ops:
  0.0 42.3 %band.1 = f32[2,128]{1,0:T(2,128)} custom-call(bf16[256,1024]{1,0:T(8,128)(2,1)} %emb_in.1, s32[256]{0:T(256)} %lab_in.1, s32[128]{0:T(128)} %req_in.1, s32[384]{0:T(512)} %pl_in.1, s32[384]{0:T(512)} %pr_in.1), custom_call_target="tpu_custom_call" | custom-call | tf_op jit(solution)/shard_map/band/pallas_call | solution.py:502
  42.3 0.0 copy-start
  42.3 0.7 %copy-done = f32[2,128]{1,0:T(2,128)S(1)} copy-done((f32[2,128]{1,0:T(2,128)S(1)}, f32[2,128]{1,0:T(2,128)}, u32[]{:S(2)}) %copy-start) | copy-done | bytes 1048
  42.9 0.6 %copy.7 = f32[256]{0:T(256)} copy(f32[256]{0:T(256)S(1)} %bitcast.1) | data formatting | bytes 2048
Async XLA Ops:
  42.3 0.7 %copy-start = (f32[2,128]{1,0:T(2,128)S(1)}, f32[2,128]{1,0:T(2,128)}, u32[]{:S(2)}) copy-start(f32[2,128]{1,0:T(2,128)} %band.1) | copy-start | bytes 3076
